TPU v7x, 32 devices: a whole 2x2x4 slice. The times are simulated.
32 devices in a mesh: dp: 8 (over z, core), tensor: 4 (over y, x).
Axes of the slice: x: 2, y: 2, z: 4, core: 2. Of those that a mesh axis runs over, the one named last changes fastest.
Arguments:
- tokens: bfloat16 [16384, 1024], P(('dp', 'tensor')), may hold values from -6 to 6
- first_values: bfloat16 [16384, 1024], P(('dp', 'tensor')), may hold values from -10 to 10
- doc_lengths: int32 [8, 8], P('dp'), may hold values from 1 to 1024, 2048 in all within a row
- attention_norm_gain: float32 [1024], replicated, may hold values from 0.5 to 1.5
- w_qkv: bfloat16 [1024, 3072], P(None, 'tensor'), may hold values from -0.1875 to 0.1875
- w_out: bfloat16 [1024, 1024], P('tensor'), may hold values from -2 to 2
- feedforward_norm_gain: float32 [1024], replicated, may hold values from 0.5 to 1.5
- w_gate: bfloat16 [1024, 2816], P(None, 'tensor'), may hold values from -0.1875 to 0.1875
- w_up: bfloat16 [1024, 2816], P(None, 'tensor'), may hold values from -0.1875 to 0.1875
- w_down: bfloat16 [2816, 1024], P('tensor'), may hold values from -0.109375 to 0.109375
- out_grad: bfloat16 [16384, 1024], P(('dp', 'tensor')), may hold values from -6 to 6
Outputs:
- out: bfloat16 [16384, 1024], P(('dp', 'tensor'))
- tokens_grad: float32 [16384, 1024], P(('dp', 'tensor'))
- first_values_grad: float32 [16384, 1024], P(('dp', 'tensor'))
- attn_gain_grad: float32 [1024], replicated
- w_qkv_grad: float32 [1024, 3072], P('dp', 'tensor')
- w_out_grad: float32 [1024, 1024], P('tensor', 'dp')
- ffn_gain_grad: float32 [1024], replicated
- w_gate_grad: float32 [1024, 2816], P('dp', 'tensor')
- w_up_grad: float32 [1024, 2816], P('dp', 'tensor')
- w_down_grad: float32 [2816, 1024], P('tensor', 'dp')
- first_values_rms: float32 [], replicated
- values_rms: float32 [], replicated
Inputs may be any that keep to these rules, and one draw needn't show every extreme that they name: `doc_lengths`: the lengths of a row sum to 2048, and its longest document has 1024 tokens.
All inputs are finite; a program needn't handle non-finite values.
Results may differ from a plain program's by a relative error of at most 0.023.
Values may be sent and summed in bfloat16 or wider, within the bound.
No kernel may reach another device: no remote copies, remote signals or barrier semaphores. Data moves between devices by JAX's collectives and lax.ppermute only.
A program may use at most 192 MiB of HBM per device.

v0:
```python
import math

import jax
import jax.numpy as jnp
from jax import lax
from jax.sharding import PartitionSpec as P

HD = 64


EPS = 1e-06


def rope_tables(length, head_width):
    half_width = head_width // 2
    inverse = jnp.exp(-math.log(10000.0) * jnp.arange(half_width, dtype=jnp.float32) / half_width)
    angles = jnp.arange(length, dtype=jnp.float32)[:, None] * inverse[None, :]
    return (jnp.cos(angles), jnp.sin(angles))


def rotate(vectors, cosine, sine_table):
    half_width = vectors.shape[-1] // 2
    first_half = vectors[..., :half_width]
    second_half = vectors[..., half_width:]
    cos_b = cosine[:, None, :]
    sin_b = sine_table[:, None, :]
    return jnp.concatenate(
        [first_half * cos_b - second_half * sin_b, first_half * sin_b + second_half * cos_b],
        axis=-1,
    )


def rotate_back(incoming, cosine, sine_table):
    half_width = incoming.shape[-1] // 2
    first_half = incoming[..., :half_width]
    second_half = incoming[..., half_width:]
    cos_b = cosine[:, None, :]
    sin_b = sine_table[:, None, :]
    return jnp.concatenate(
        [first_half * cos_b + second_half * sin_b, second_half * cos_b - first_half * sin_b],
        axis=-1,
    )


def document_ids(lengths, length):
    doc_ends = jnp.cumsum(lengths, axis=-1)
    places = jnp.arange(length, dtype=jnp.int32)
    return jnp.sum((places[None, :, None] >= doc_ends[:, None, :]).astype(jnp.int32), axis=-1)


def allowed_block(doc_row, begin_row, block_rows):
    key_places = jnp.arange(doc_row.shape[0], dtype=jnp.int32)
    query_places = begin_row + jnp.arange(block_rows, dtype=jnp.int32)
    query_docs = lax.dynamic_slice_in_dim(doc_row, begin_row, block_rows, 0)
    return (query_docs[:, None] == doc_row[None, :]) & (
        query_places[:, None] >= key_places[None, :]
    )


def rms_normalize(row_block):
    inverse = lax.rsqrt(jnp.mean(row_block * row_block, axis=-1, keepdims=True) + EPS)
    return (row_block * inverse, inverse)


def rms_normalize_backward(normed, inverse, gain_vec, incoming):
    scaled = incoming * gain_vec
    inner_mean = jnp.mean(scaled * normed, axis=-1, keepdims=True)
    return (inverse * (scaled - normed * inner_mean), jnp.sum(incoming * normed, axis=0))


def shards(
    tokens,
    first_values,
    doc_lengths,
    attention_norm_gain,
    w_qkv,
    w_out,
    feedforward_norm_gain,
    w_gate,
    w_up,
    w_down,
    out_grad,
):
    local_rows = tokens.shape[0]
    row_count = doc_lengths.shape[0]
    local_heads = w_out.shape[0] // HD
    total_rows = local_rows * lax.axis_size("tensor")
    length = total_rows // row_count
    block_rows = min(512, length)
    block_count = length // block_rows
    score_scale = HD ** (-0.5)
    cosine, sine_table = rope_tables(length, HD)
    doc_table = document_ids(doc_lengths, length)
    residual_input = tokens.astype(jnp.float32)
    first_unit_rows, first_inverse_rms = rms_normalize(residual_input)
    first_normed_rows = (first_unit_rows * attention_norm_gain).astype(jnp.bfloat16)
    normed_all = lax.all_gather(first_normed_rows, "tensor", axis=0, tiled=True)
    first_local = lax.all_to_all(first_values, "tensor", split_axis=1, concat_axis=0, tiled=True)
    projected = jnp.dot(normed_all, w_qkv, preferred_element_type=jnp.float32).reshape(
        row_count, length, local_heads, 3, HD
    )
    queries = rotate(projected[:, :, :, 0], cosine, sine_table).astype(jnp.bfloat16)
    key_rows = rotate(projected[:, :, :, 1], cosine, sine_table).astype(jnp.bfloat16)
    mixed_values = 0.5 * projected[:, :, :, 2] + 0.5 * first_local.astype(jnp.float32).reshape(
        row_count, length, local_heads, HD
    )
    value_rows = mixed_values.astype(jnp.bfloat16)

    def attend_row(row_items):
        query_row, key_row, value_row, doc_row = row_items

        def attend_block(block_index):
            begin_row = block_index * block_rows
            query_part = lax.dynamic_slice_in_dim(query_row, begin_row, block_rows, 0)
            scores = (
                jnp.einsum("qhd,khd->hqk", query_part, key_row, preferred_element_type=jnp.float32)
                * score_scale
            )
            scores = jnp.where(allowed_block(doc_row, begin_row, block_rows)[None], scores, -1e30)
            row_max = jnp.max(scores, axis=-1, keepdims=True)
            weights = jnp.exp(scores - row_max)
            row_total = jnp.sum(weights, axis=-1, keepdims=True)
            probabilities = weights / row_total
            block_out = jnp.einsum(
                "hqk,khd->qhd",
                probabilities.astype(jnp.bfloat16),
                value_row,
                preferred_element_type=jnp.float32,
            )
            return (block_out, (row_max + jnp.log(row_total))[..., 0])

        block_outs, logsums = lax.map(attend_block, jnp.arange(block_count))
        return (block_outs.reshape(length, local_heads, HD), logsums)

    attended_rows, logsum_table = lax.map(attend_row, (queries, key_rows, value_rows, doc_table))
    attended = attended_rows.reshape(total_rows, local_heads * HD).astype(jnp.bfloat16)
    row_block_part = attended
    middle_stream = residual_input + lax.psum_scatter(
        jnp.dot(row_block_part, w_out, preferred_element_type=jnp.float32).astype(jnp.bfloat16),
        "tensor",
        scatter_dimension=0,
        tiled=True,
    ).astype(jnp.float32)
    second_unit_rows, second_inverse_rms = rms_normalize(middle_stream)
    second_normed_rows = (second_unit_rows * feedforward_norm_gain).astype(jnp.bfloat16)
    gate_full, up_full, down_full = (w_gate, w_up, w_down)
    ffn_input = lax.all_gather(second_normed_rows, "tensor", axis=0, tiled=True)
    gate_act = jnp.dot(ffn_input, gate_full, preferred_element_type=jnp.float32)
    up_act = jnp.dot(ffn_input, up_full, preferred_element_type=jnp.float32)
    sigmoid_gate = jax.nn.sigmoid(gate_act)
    hidden = (gate_act * sigmoid_gate * up_act).astype(jnp.bfloat16)
    row_block_part = hidden
    ffn_out = lax.psum_scatter(
        jnp.dot(row_block_part, down_full, preferred_element_type=jnp.float32).astype(jnp.bfloat16),
        "tensor",
        scatter_dimension=0,
        tiled=True,
    ).astype(jnp.float32)
    out = (middle_stream + ffn_out).astype(jnp.bfloat16)
    out_rows = lax.all_gather(out_grad, "tensor", axis=0, tiled=True)
    down_grad = jnp.einsum("tf,td->fd", hidden, out_rows, preferred_element_type=jnp.float32)
    d_hidden = jnp.einsum("td,fd->tf", out_rows, down_full, preferred_element_type=jnp.float32)
    d_up = (d_hidden * gate_act * sigmoid_gate).astype(jnp.bfloat16)
    d_gate = (d_hidden * up_act * sigmoid_gate * (1.0 + gate_act * (1.0 - sigmoid_gate))).astype(
        jnp.bfloat16
    )
    gate_grad = jnp.einsum("td,tf->df", ffn_input, d_gate, preferred_element_type=jnp.float32)
    up_grad = jnp.einsum("td,tf->df", ffn_input, d_up, preferred_element_type=jnp.float32)
    second_normed_cotangent = lax.psum_scatter(
        (
            jnp.einsum("tf,df->td", d_gate, gate_full, preferred_element_type=jnp.float32)
            + jnp.einsum("tf,df->td", d_up, up_full, preferred_element_type=jnp.float32)
        ).astype(jnp.bfloat16),
        "tensor",
        scatter_dimension=0,
        tiled=True,
    ).astype(jnp.float32)
    middle_norm_cotangent, feedforward_gain_share = rms_normalize_backward(
        second_unit_rows, second_inverse_rms, feedforward_norm_gain, second_normed_cotangent
    )
    d_middle = out_grad.astype(jnp.float32) + middle_norm_cotangent
    d_branch = lax.all_gather(d_middle.astype(jnp.bfloat16), "tensor", axis=0, tiled=True)
    out_weight_grad = jnp.einsum(
        "te,td->ed", attended, d_branch, preferred_element_type=jnp.float32
    )
    d_attended = (
        jnp.einsum("td,ed->te", d_branch, w_out, preferred_element_type=jnp.float32)
        .astype(jnp.bfloat16)
        .reshape(row_count, length, local_heads, HD)
    )

    def attend_back_row(row_items):
        query_row, key_row, value_row, doc_row, logsum_row, grad_row = row_items

        def back_block(scan_state, block_index):
            key_acc, value_acc = scan_state
            begin_row = block_index * block_rows
            query_part = lax.dynamic_slice_in_dim(query_row, begin_row, block_rows, 0)
            grad_part = lax.dynamic_slice_in_dim(grad_row, begin_row, block_rows, 0)
            scores = (
                jnp.einsum("qhd,khd->hqk", query_part, key_row, preferred_element_type=jnp.float32)
                * score_scale
            )
            scores = jnp.where(allowed_block(doc_row, begin_row, block_rows)[None], scores, -1e30)
            probabilities = jnp.exp(scores - logsum_row[block_index][..., None])
            d_prob = jnp.einsum(
                "qhd,khd->hqk", grad_part, value_row, preferred_element_type=jnp.float32
            )
            centre = jnp.sum(d_prob * probabilities, axis=-1, keepdims=True)
            d_scores = (probabilities * (d_prob - centre)).astype(jnp.bfloat16)
            d_query = (
                jnp.einsum("hqk,khd->qhd", d_scores, key_row, preferred_element_type=jnp.float32)
                * score_scale
            )
            key_acc = (
                key_acc
                + jnp.einsum(
                    "hqk,qhd->khd", d_scores, query_part, preferred_element_type=jnp.float32
                )
                * score_scale
            )
            value_acc = value_acc + jnp.einsum(
                "hqk,qhd->khd",
                probabilities.astype(jnp.bfloat16),
                grad_part,
                preferred_element_type=jnp.float32,
            )
            return ((key_acc, value_acc), d_query)

        empty_acc = jnp.zeros((length, local_heads, HD), jnp.float32)
        (key_grad, value_grad), query_grad = lax.scan(
            back_block, (empty_acc, empty_acc), jnp.arange(block_count)
        )
        return (query_grad.reshape(length, local_heads, HD), key_grad, value_grad)

    query_grads, key_grads, value_grads = lax.map(
        attend_back_row, (queries, key_rows, value_rows, doc_table, logsum_table, d_attended)
    )
    d_queries = rotate_back(query_grads, cosine, sine_table).astype(jnp.bfloat16)
    d_keys = rotate_back(key_grads, cosine, sine_table).astype(jnp.bfloat16)
    d_half = (value_grads.astype(jnp.bfloat16).astype(jnp.float32) * 0.5).astype(jnp.bfloat16)
    d_qkv = jnp.stack([d_queries, d_keys, d_half], axis=3).reshape(total_rows, 3 * local_heads * HD)
    qkv_grad = jnp.einsum("tc,te->ce", normed_all, d_qkv, preferred_element_type=jnp.float32)
    row_block_part = d_qkv
    first_normed_cotangent = lax.psum_scatter(
        jnp.einsum("te,ce->tc", row_block_part, w_qkv, preferred_element_type=jnp.float32).astype(
            jnp.bfloat16
        ),
        "tensor",
        scatter_dimension=0,
        tiled=True,
    ).astype(jnp.float32)
    first_grad = lax.all_to_all(
        d_half.reshape(total_rows, local_heads * HD),
        "tensor",
        split_axis=0,
        concat_axis=1,
        tiled=True,
    ).astype(jnp.float32)
    input_norm_cotangent, attention_gain_share = rms_normalize_backward(
        first_unit_rows, first_inverse_rms, attention_norm_gain, first_normed_cotangent
    )
    tokens_grad = d_middle + input_norm_cotangent
    reduced = (
        lax.psum_scatter(
            qkv_grad.astype(jnp.bfloat16), "dp", scatter_dimension=0, tiled=True
        ).astype(jnp.float32),
        lax.psum_scatter(
            out_weight_grad.astype(jnp.bfloat16), "dp", scatter_dimension=1, tiled=True
        ).astype(jnp.float32),
        lax.psum_scatter(
            gate_grad.astype(jnp.bfloat16), "dp", scatter_dimension=0, tiled=True
        ).astype(jnp.float32),
        lax.psum_scatter(
            up_grad.astype(jnp.bfloat16), "dp", scatter_dimension=0, tiled=True
        ).astype(jnp.float32),
        lax.psum_scatter(
            down_grad.astype(jnp.bfloat16), "dp", scatter_dimension=1, tiled=True
        ).astype(jnp.float32),
    )
    first_all = first_values.astype(jnp.float32)
    first_squares = jnp.sum(first_all * first_all)
    mixed_squares = jnp.sum(mixed_values * mixed_values)
    attn_gain_grad, ffn_gain_grad, first_total, mixed_total = lax.psum(
        (attention_gain_share, feedforward_gain_share, first_squares, mixed_squares),
        ("dp", "tensor"),
    )
    entry_count = first_values.size * lax.axis_size("dp") * lax.axis_size("tensor")
    return (
        out,
        tokens_grad,
        first_grad,
        attn_gain_grad,
        reduced[0],
        reduced[1],
        ffn_gain_grad,
        reduced[2],
        reduced[3],
        reduced[4],
        jnp.sqrt(first_total / entry_count),
        jnp.sqrt(mixed_total / entry_count),
    )


def solution(mesh):
    return jax.shard_map(
        shards,
        mesh=mesh,
        in_specs=(
            P(("dp", "tensor"), None),
            P(("dp", "tensor"), None),
            P("dp", None),
            P(),
            P(None, "tensor"),
            P("tensor", None),
            P(),
            P(None, "tensor"),
            P(None, "tensor"),
            P("tensor", None),
            P(("dp", "tensor"), None),
        ),
        out_specs=(
            P(("dp", "tensor"), None),
            P(("dp", "tensor"), None),
            P(("dp", "tensor"), None),
            P(),
            P("dp", "tensor"),
            P("tensor", "dp"),
            P(),
            P("dp", "tensor"),
            P("dp", "tensor"),
            P("tensor", "dp"),
            P(),
            P(),
        ),
        check_vma=False,
    )
```

profile of v0, /device:TPU:0, one launch (start us, length us, event | category | flops | bytes accessed | tf_op | source)
XLA Modules:
  0.0 923.4 jit_solution(6048595664378396844)
XLA Ops:
  13.4 5.2 all-to-all-start
  19.9 20.4 %all-to-all-done = bf16[512,4,256]{0,2,1:T(8,128)(2,1)S(1)} async-done(((bf16[512,4,256]{0,2,1:T(8,128)(2,1)}), bf16[512,4,256]{0,2,1:T(8,128)(2,1)S(1)}, u32[]{:S(2)}, u32[]{:S(2)}) %all-to-all-start) | async-done | bytes 1048608 | tf_op jit(solution)/shard_map/all_to_all | solution.py:98
  47.0 27.2 %all-gather.5.cloned.1.call-done = bf16[2048,1024]{1,0:T(8,128)(2,1)} async-done(((bf16[512,1024]{1,0:T(8,128)(2,1)}), bf16[2048,1024]{1,0:T(8,128)(2,1)}) %all-gather.5.cloned.1.call-update) | async-done | bytes 4194320 | tf_op jit(solution)/shard_map/all_gather | solution.py:97
  74.2 5.4 fusion.71
  86.1 68.8 %while.47 = (s32[]{:T(128)}, bf16[4,512,4,64]{1,3,2,0:T(8,128)(2,1)}, f32[4,4,512]{2,1,0:T(4,128)S(1)}, s32[4]{0:T(128)S(1)}, s32[2048]{0:T(1024)S(1)}, /*index=...) while((s32[]{:T(128)}, ...), condition=%wide.region_6.7_spmd, body=%wide.region_3.6_spmd.sunk | while | flops 1127217664 | bytes 70076696 | solution.py:132
  97.4 4.8 fusion.138
  114.5 4.8 fusion.138
  131.6 4.8 fusion.138
  148.8 4.8 fusion.138
  161.6 52.8 %reduce-scatter.18.cloned.1.call-done = bf16[512,1024]{1,0:T(8,128)(2,1)} async-done(((bf16[2048,1024]{1,0:T(8,128)(2,1)}), bf16[512,1024]{1,0:T(8,128)(2,1)}) %reduce-scatter.18.cloned.1.call-update) | async-done | bytes 1048592 | tf_op jit(solution)/shard_map/reduce_scatter | solution.py:138
  220.0 52.2 %all-gather.7.cloned.1.call-done = bf16[2048,1024]{1,0:T(8,128)(2,1)} async-done(((bf16[512,1024]{1,0:T(8,128)(2,1)}), bf16[2048,1024]{1,0:T(8,128)(2,1)}) %all-gather.7.cloned.1.call-update) | async-done | bytes 4194320 | tf_op jit(solution)/shard_map/all_gather | solution.py:147
  272.2 8.5 fusion.73
  280.7 5.0 fusion.72
  285.6 41.1 %all-gather.9.cloned.1.call-done = bf16[2048,1024]{1,0:T(8,128)(2,1)} async-done(((bf16[512,1024]{1,0:T(8,128)(2,1)}), bf16[2048,1024]{1,0:T(8,128)(2,1)}) %all-gather.9.cloned.1.call-update) | async-done | bytes 4194320 | tf_op jit(solution)/shard_map/all_gather | solution.py:160
  326.8 11.8 %multiply_convert_fusion.1 = (bf16[2048,704]{0,1:T(8,128)(2,1)S(1)}, bf16[2048,704]{0,1:T(8,128)(2,1)S(1)}, bf16[2048,704]{0,1:T(8,128)(2,1)}) fusion(f32[2048,704]{0,1:T(8,128)} %fusion.72, f32[2048,704]{0,1:T(8,128)} %fusion.73, bf16[2048,1024]{1,0:T(8,128)(2,1)} %all-gather.9.cloned.1.call-done, bf16[704,1024]{1,0:T(8,128)(2,1)} %param.24), kind=kOutput, calls=%fused_computation.47 | convolution fusion | flops 2975858688 | bytes 25821184 | tf_op jit(solution)/shard_map/td,fd->tf/dot_general | solution.py:162
  342.1 5.0 add_convert_fusion
  347.2 52.8 %reduce-scatter.22.cloned.1.call-done = bf16[512,1024]{1,0:T(8,128)(2,1)} async-done(((bf16[2048,1024]{1,0:T(8,128)(2,1)}), bf16[512,1024]{1,0:T(8,128)(2,1)}) %reduce-scatter.22.cloned.1.call-update) | async-done | bytes 1048592 | tf_op jit(solution)/shard_map/reduce_scatter | solution.py:169
  407.5 7.3 convolution_convert_fusion.7
  417.5 7.3 convolution_convert_fusion.5
  427.5 7.3 convolution_convert_fusion.6
  437.9 22.2 %all-gather.11.cloned.1.call-done = bf16[2048,1024]{1,0:T(8,128)(2,1)} async-done(((bf16[512,1024]{1,0:T(8,128)(2,1)}), bf16[2048,1024]{1,0:T(8,128)(2,1)}) %all-gather.11.cloned.1.call-update) | async-done | bytes 4194320 | tf_op jit(solution)/shard_map/all_gather | solution.py:182
  464.5 259.3 %while.48 = (s32[]{:T(128)}, f32[2048,4,64]{0,2,1:T(8,128)}, f32[2048,4,64]{0,2,1:T(8,128)}, f32[4,512,4,64]{1,0,3,2:T(4,128)}, s32[4]{0:T(128)S(1)}, /*index=5*...) while((s32[]{:T(128)}, f32[2048,4,64]{0,2,1:T(8,128)}, ...), condition=%wide.region_14.15_spmd.clone, body=%wide.region_12.14_spmd.clone.sunk | while | flops 2753165824 | bytes 212412720 | solution.py:231
  472.6 5.7 copy-done.1
  478.3 7.1 fusion.151
  485.4 12.8 %multiply_reduce_fusion.4 = (f32[4,512]{1,0:T(4,128)S(1)}, f32[4,512,2048]{2,1,0:T(8,128)}) fusion(f32[4,512,2048]{2,1,0:T(8,128)} %copy-done.1, f32[4,512]{1,0:T(4,128)S(1)} %dynamic-slice_bitcast_fusion.2, pred[512,2048]{1,0:T(8,128)(4,1)S(1)} %fusion.149, bf16[2048,4,64]{0,2,1:T(8,128)(2,1)} %get-tuple-element.505, ...), kind=kOutput, calls=%fused_computation.18.clone.1 | convolution fusion | flops 557840384 | bytes 35930116 | tf_op jit(solution)/shard_map/while/body/eval_jaxpr/while/body/eval_jaxpr/qhd,khd->hqk/dot_general | solution.py:206
  498.2 12.3 %multiply_convert_fusion.7 = bf16[4,512,2048]{2,1,0:T(8,128)(2,1)S(1)} fusion(f32[4,512,2048]{2,1,0:T(8,128)} %get-tuple-element.425, f32[4,512,2048]{2,1,0:T(8,128)} %copy-done.1, f32[4,512]{1,0:T(4,128)S(1)} %get-tuple-element.426, f32[4,512]{1,0:T(4,128)S(1)} %dynamic-slice_bitcast_fusion.2, pred[512,2048]{1,0:T(8,128)(4,1)S(1)} %fusion.149), kind=kLoop, calls=%fused_computation.17.clone.1 | loop fusion | flops 25165824 | bytes 43008000 | tf_op jit(solution)/shard_map/while/body/eval_jaxpr/while/body/eval_jaxpr/convert_element_type | solution.py:210
  517.6 11.1 %dynamic_update_slice.31 = f32[4,512,4,64]{1,0,3,2:T(4,128)} dynamic-update-slice(f32[4,512,4,64]{1,0,3,2:T(4,128)} %get-tuple-element.482, f32[1,512,4,64]{1,0,3,2:T(1,128)S(1)} %copy.81, s32[]{:T(128)S(6)} %copy.98, s32[]{:T(128)} %constant.102.clone.1..sunk.1, s32[]{:T(128)} %constant.102.clone.1..sunk.1, s32[]{:T(128)} %constant.102.clone.1..sunk.1) | dynamic-update-slice | bytes 1048580 | tf_op jit(solution)/shard_map/while/body/eval_jaxpr/while/body/jit(dynamic_update_index_in_dim)/dynamic_update_slice | solution.py:132
  536.5 5.7 copy-done.1
  542.2 7.5 fusion.151
  549.8 12.9 %multiply_reduce_fusion.4 = (f32[4,512]{1,0:T(4,128)S(1)}, f32[4,512,2048]{2,1,0:T(8,128)}) fusion(f32[4,512,2048]{2,1,0:T(8,128)} %copy-done.1, f32[4,512]{1,0:T(4,128)S(1)} %dynamic-slice_bitcast_fusion.2, pred[512,2048]{1,0:T(8,128)(4,1)S(1)} %fusion.149, bf16[2048,4,64]{0,2,1:T(8,128)(2,1)} %get-tuple-element.505, ...), kind=kOutput, calls=%fused_computation.18.clone.1 | convolution fusion | flops 557840384 | bytes 35930116 | tf_op jit(solution)/shard_map/while/body/eval_jaxpr/while/body/eval_jaxpr/qhd,khd->hqk/dot_general | solution.py:206
  562.7 12.2 %multiply_convert_fusion.7 = bf16[4,512,2048]{2,1,0:T(8,128)(2,1)S(1)} fusion(f32[4,512,2048]{2,1,0:T(8,128)} %get-tuple-element.425, f32[4,512,2048]{2,1,0:T(8,128)} %copy-done.1, f32[4,512]{1,0:T(4,128)S(1)} %get-tuple-element.426, f32[4,512]{1,0:T(4,128)S(1)} %dynamic-slice_bitcast_fusion.2, pred[512,2048]{1,0:T(8,128)(4,1)S(1)} %fusion.149), kind=kLoop, calls=%fused_computation.17.clone.1 | loop fusion | flops 25165824 | bytes 43008000 | tf_op jit(solution)/shard_map/while/body/eval_jaxpr/while/body/eval_jaxpr/convert_element_type | solution.py:210
  582.7 11.1 %dynamic_update_slice.31 = f32[4,512,4,64]{1,0,3,2:T(4,128)} dynamic-update-slice(f32[4,512,4,64]{1,0,3,2:T(4,128)} %get-tuple-element.482, f32[1,512,4,64]{1,0,3,2:T(1,128)S(1)} %copy.81, s32[]{:T(128)S(6)} %copy.98, s32[]{:T(128)} %constant.102.clone.1..sunk.1, s32[]{:T(128)} %constant.102.clone.1..sunk.1, s32[]{:T(128)} %constant.102.clone.1..sunk.1) | dynamic-update-slice | bytes 1048580 | tf_op jit(solution)/shard_map/while/body/eval_jaxpr/while/body/jit(dynamic_update_index_in_dim)/dynamic_update_slice | solution.py:132
  601.6 5.7 copy-done.1
  607.3 7.5 fusion.151
  614.8 12.8 %multiply_reduce_fusion.4 = (f32[4,512]{1,0:T(4,128)S(1)}, f32[4,512,2048]{2,1,0:T(8,128)}) fusion(f32[4,512,2048]{2,1,0:T(8,128)} %copy-done.1, f32[4,512]{1,0:T(4,128)S(1)} %dynamic-slice_bitcast_fusion.2, pred[512,2048]{1,0:T(8,128)(4,1)S(1)} %fusion.149, bf16[2048,4,64]{0,2,1:T(8,128)(2,1)} %get-tuple-element.505, ...), kind=kOutput, calls=%fused_computation.18.clone.1 | convolution fusion | flops 557840384 | bytes 35930116 | tf_op jit(solution)/shard_map/while/body/eval_jaxpr/while/body/eval_jaxpr/qhd,khd->hqk/dot_general | solution.py:206
  627.6 12.1 %multiply_convert_fusion.7 = bf16[4,512,2048]{2,1,0:T(8,128)(2,1)S(1)} fusion(f32[4,512,2048]{2,1,0:T(8,128)} %get-tuple-element.425, f32[4,512,2048]{2,1,0:T(8,128)} %copy-done.1, f32[4,512]{1,0:T(4,128)S(1)} %get-tuple-element.426, f32[4,512]{1,0:T(4,128)S(1)} %dynamic-slice_bitcast_fusion.2, pred[512,2048]{1,0:T(8,128)(4,1)S(1)} %fusion.149), kind=kLoop, calls=%fused_computation.17.clone.1 | loop fusion | flops 25165824 | bytes 43008000 | tf_op jit(solution)/shard_map/while/body/eval_jaxpr/while/body/eval_jaxpr/convert_element_type | solution.py:210
  647.6 11.1 %dynamic_update_slice.31 = f32[4,512,4,64]{1,0,3,2:T(4,128)} dynamic-update-slice(f32[4,512,4,64]{1,0,3,2:T(4,128)} %get-tuple-element.482, f32[1,512,4,64]{1,0,3,2:T(1,128)S(1)} %copy.81, s32[]{:T(128)S(6)} %copy.98, s32[]{:T(128)} %constant.102.clone.1..sunk.1, s32[]{:T(128)} %constant.102.clone.1..sunk.1, s32[]{:T(128)} %constant.102.clone.1..sunk.1) | dynamic-update-slice | bytes 1048580 | tf_op jit(solution)/shard_map/while/body/eval_jaxpr/while/body/jit(dynamic_update_index_in_dim)/dynamic_update_slice | solution.py:132
  666.5 5.7 copy-done.1
  672.2 7.5 fusion.151
  679.7 12.8 %multiply_reduce_fusion.4 = (f32[4,512]{1,0:T(4,128)S(1)}, f32[4,512,2048]{2,1,0:T(8,128)}) fusion(f32[4,512,2048]{2,1,0:T(8,128)} %copy-done.1, f32[4,512]{1,0:T(4,128)S(1)} %dynamic-slice_bitcast_fusion.2, pred[512,2048]{1,0:T(8,128)(4,1)S(1)} %fusion.149, bf16[2048,4,64]{0,2,1:T(8,128)(2,1)} %get-tuple-element.505, ...), kind=kOutput, calls=%fused_computation.18.clone.1 | convolution fusion | flops 557840384 | bytes 35930116 | tf_op jit(solution)/shard_map/while/body/eval_jaxpr/while/body/eval_jaxpr/qhd,khd->hqk/dot_general | solution.py:206
  692.5 12.1 %multiply_convert_fusion.7 = bf16[4,512,2048]{2,1,0:T(8,128)(2,1)S(1)} fusion(f32[4,512,2048]{2,1,0:T(8,128)} %get-tuple-element.425, f32[4,512,2048]{2,1,0:T(8,128)} %copy-done.1, f32[4,512]{1,0:T(4,128)S(1)} %get-tuple-element.426, f32[4,512]{1,0:T(4,128)S(1)} %dynamic-slice_bitcast_fusion.2, pred[512,2048]{1,0:T(8,128)(4,1)S(1)} %fusion.149), kind=kLoop, calls=%fused_computation.17.clone.1 | loop fusion | flops 25165824 | bytes 43008000 | tf_op jit(solution)/shard_map/while/body/eval_jaxpr/while/body/eval_jaxpr/convert_element_type | solution.py:210
  712.4 11.1 %dynamic_update_slice.31 = f32[4,512,4,64]{1,0,3,2:T(4,128)} dynamic-update-slice(f32[4,512,4,64]{1,0,3,2:T(4,128)} %get-tuple-element.482, f32[1,512,4,64]{1,0,3,2:T(1,128)S(1)} %copy.81, s32[]{:T(128)S(6)} %copy.98, s32[]{:T(128)} %constant.102.clone.1..sunk.1, s32[]{:T(128)} %constant.102.clone.1..sunk.1, s32[]{:T(128)} %constant.102.clone.1..sunk.1) | dynamic-update-slice | bytes 1048580 | tf_op jit(solution)/shard_map/while/body/eval_jaxpr/while/body/jit(dynamic_update_index_in_dim)/dynamic_update_slice | solution.py:132
  745.6 7.0 convolution_convert_fusion.2
  752.7 7.8 convolution_convert_fusion
  791.2 9.1 reduce-scatter.26.cloned.1.call-done
  802.1 51.8 %reduce-scatter.24.cloned.1.call-done = bf16[512,1024]{1,0:T(8,128)(2,1)} async-done(((bf16[2048,1024]{1,0:T(8,128)(2,1)}), bf16[512,1024]{1,0:T(8,128)(2,1)}) %reduce-scatter.24.cloned.1.call-update) | async-done | bytes 1048592 | tf_op jit(solution)/shard_map/reduce_scatter | solution.py:245
  855.9 39.8 %all-reduce = (f32[1024]{0:T(1024)}, f32[1024]{0:T(1024)}, f32[]{:T(128)}, f32[]{:T(128)}) all-reduce(f32[1024]{0:T(1024)S(1)} %get-tuple-element.232, f32[1024]{0:T(1024)S(1)} %copy-done.28, f32[]{:T(128)} %multiply_reduce_fusion.1, f32[]{:T(128)} %fusion.56), channel_id=1, replica_groups=mesh['dp'=8,'tensor'=4] {'dp','tensor'}, use_global_device_ids=true, to_apply=%region_18.19 | all-reduce | flops 2050 | bytes 16400 | tf_op jit(solution)/shard_map/psum | solution.py:284
  897.1 12.7 %reduce-scatter.20.cloned.1.call-done = bf16[512,1024]{1,0:T(8,128)(2,1)} async-done(((bf16[2048,1024]{1,0:T(8,128)(2,1)}), bf16[512,1024]{1,0:T(8,128)(2,1)}) %reduce-scatter.20.cloned.1.call-update) | async-done | bytes 1048592 | tf_op jit(solution)/shard_map/reduce_scatter | solution.py:153
  (254 shorter events, 215.0 us)
Async XLA Ops:
  7.2 67.0 %copy-start = (bf16[1024,768]{1,0:T(8,128)(2,1)S(1)}, bf16[1024,768]{1,0:T(8,128)(2,1)}, u32[]{:S(2)}) copy-start(bf16[1024,768]{1,0:T(8,128)(2,1)} %param.19) | copy-start | bytes 4718596
  7.2 4.8 copy-start.10
  7.2 67.0 %all-gather.5.cloned.1.call-start = ((), (), s32[]{:S(2)}) async-start(), calls=%async_computation.11 | async-start | bytes 5242880 | tf_op jit(solution)/shard_map/all_gather | solution.py:97
  12.0 6.5 copy-start.34
  13.4 26.9 %all-to-all-start = ((bf16[512,4,256]{0,2,1:T(8,128)(2,1)}), bf16[512,4,256]{0,2,1:T(8,128)(2,1)S(1)}, u32[]{:S(2)}, u32[]{:S(2)}) async-start(bf16[512,4,256]{0,2,1:T(8,128)(2,1)} %bitcast.171), calls=%async_computation | async-start | bytes 2097152 | tf_op jit(solution)/shard_map/all_to_all | solution.py:98
  18.5 195.9 %reduce-scatter.18.cloned.1.call-start = ((), (), s32[]{:S(2)}) async-start(), calls=%async_computation.12 | async-start | bytes 5242880 | tf_op jit(solution)/shard_map/reduce_scatter | solution.py:138
  19.8 64.3 %copy-start.12 = (f32[2048,32]{0,1:T(8,128)}, f32[2048,32]{0,1:T(8,128)S(1)}, u32[]{:S(2)}) copy-start(f32[2048,32]{0,1:T(8,128)S(1)} %get-tuple-element.299) | copy-start | bytes 786436
  19.8 64.3 %copy-start.14 = (f32[2048,32]{0,1:T(8,128)}, f32[2048,32]{0,1:T(8,128)S(1)}, u32[]{:S(2)}) copy-start(f32[2048,32]{0,1:T(8,128)S(1)} %get-tuple-element.300) | copy-start | bytes 786436
  93.1 4.4 copy-start.4
  93.1 4.4 copy-start.16
  110.2 4.4 copy-start.4
  110.2 4.4 copy-start.16
  127.3 4.4 copy-start.4
  127.3 4.4 copy-start.16
  144.4 4.4 copy-start.4
  144.4 4.4 copy-start.16
  161.5 54.9 %copy-start.19 = (f32[1024]{0:T(1024)S(1)}, f32[1024]{0:T(1024)}, u32[]{:S(2)}) copy-start(f32[1024]{0:T(1024)} %param.21) | copy-start | bytes 12292
  161.6 110.6 %all-gather.7.cloned.1.call-start = ((), (), s32[]{:S(2)}) async-start(), calls=%async_computation.13 | async-start | bytes 5242880 | tf_op jit(solution)/shard_map/all_gather | solution.py:147
  216.4 187.2 %copy-start.21 = (f32[512]{0:T(512)}, f32[512]{0:T(512)S(1)}, u32[]{:S(2)}) copy-start(f32[512]{0:T(512)S(1)} %add_rsqrt_fusion) | copy-start | bytes 6148
  219.3 107.4 %all-gather.9.cloned.1.call-start = ((), (), s32[]{:S(2)}) async-start(), calls=%async_computation.15 | async-start | bytes 5242880 | tf_op jit(solution)/shard_map/all_gather | solution.py:160
  219.9 180.1 %reduce-scatter.22.cloned.1.call-start = ((), (), s32[]{:S(2)}) async-start(), calls=%async_computation.16 | async-start | bytes 5242880 | tf_op jit(solution)/shard_map/reduce_scatter | solution.py:169
  272.2 8.5 copy-start.30
  272.2 8.5 copy-start.31
  326.8 11.8 %copy-start.32 = (bf16[1024,704]{0,1:T(8,128)(2,1)S(1)}, bf16[1024,704]{0,1:T(8,128)(2,1)}, u32[]{:S(2)}) copy-start(bf16[1024,704]{0,1:T(8,128)(2,1)} %param.22) | copy-start | bytes 4325380
  338.6 3.5 copy-start.33
  347.2 112.9 %all-gather.11.cloned.1.call-start = ((), (), s32[]{:S(2)}) async-start(), calls=%async_computation.17 | async-start | bytes 5242880 | tf_op jit(solution)/shard_map/all_gather | solution.py:182
  400.0 4.1 copy-start.2
  400.1 4.1 copy-start.5
  400.1 4.1 copy-start.7
  407.2 372.1 %reduce-scatter.34.cloned.1.call-start = ((), (), s32[]{:S(2)}) async-start(), calls=%async_computation.23 | async-start | bytes 1769472
  417.5 363.8 %reduce-scatter.32.cloned.1.call-start = ((), (), s32[]{:S(2)}) async-start(), calls=%async_computation.22 | async-start | bytes 1769472
  427.5 355.7 %reduce-scatter.30.cloned.1.call-start = ((), (), s32[]{:S(2)}) async-start(), calls=%async_computation.21 | async-start | bytes 1769472
  437.8 351.8 %reduce-scatter.28.cloned.1.call-start = ((), (), s32[]{:S(2)}) async-start(), calls=%async_computation.20 | async-start | bytes 589824
  472.5 5.7 copy-start.1
  536.5 5.7 copy-start.1
  601.6 5.7 copy-start.1
  666.4 5.7 copy-start.1
  734.2 66.2 %reduce-scatter.26.cloned.1.call-start = ((), (), s32[]{:S(2)}) async-start(), calls=%async_computation.19 | async-start | bytes 1769472 | tf_op jit(solution)/shard_map/reduce_scatter | solution.py:265
  745.6 108.3 %reduce-scatter.24.cloned.1.call-start = ((), (), s32[]{:S(2)}) async-start(), calls=%async_computation.18 | async-start | bytes 5242880 | tf_op jit(solution)/shard_map/reduce_scatter | solution.py:245
  752.7 157.2 %reduce-scatter.20.cloned.1.call-start = ((), (), s32[]{:S(2)}) async-start(), calls=%async_computation.14 | async-start | bytes 5242880 | tf_op jit(solution)/shard_map/reduce_scatter | solution.py:153
  766.3 18.7 %all-to-all-start.1 = ((bf16[4,512,256]{1,2,0:T(8,128)(2,1)}), bf16[4,512,256]{1,2,0:T(8,128)(2,1)S(1)}, u32[]{:S(2)}, u32[]{:S(2)}) async-start(bf16[4,512,256]{1,2,0:T(8,128)(2,1)} %copy.55), calls=%async_computation.5 | async-start | bytes 2097152 | tf_op jit(solution)/shard_map/all_to_all | solution.py:253
  786.6 67.3 %copy-start.3 = (bf16[512,1024]{1,0:T(8,128)(2,1)S(1)}, bf16[512,1024]{1,0:T(8,128)(2,1)}, u32[]{:S(2)}) copy-start(bf16[512,1024]{1,0:T(8,128)(2,1)} %param.15) | copy-start | bytes 3145732
  786.6 67.3 %copy-start.23 = (f32[1024]{0:T(1024)S(1)}, f32[1024]{0:T(1024)}, u32[]{:S(2)}) copy-start(f32[1024]{0:T(1024)} %param.18) | copy-start | bytes 12292
  786.6 67.3 %copy-start.25 = (f32[512]{0:T(512)S(1)}, f32[512]{0:T(512)}, u32[]{:S(2)}) copy-start(f32[512]{0:T(512)} %copy-done.24) | copy-start | bytes 6148
  786.6 69.3 %copy-start.28 = (f32[1024]{0:T(1024)S(1)}, f32[1024]{0:T(1024)}, u32[]{:S(2)}) copy-start(f32[1024]{0:T(1024)} %get-tuple-element.230) | copy-start | bytes 12292
  786.6 123.3 %copy-start.20 = (f32[1024]{0:T(1024)S(1)}, f32[1024]{0:T(1024)}, u32[]{:S(2)}) copy-start(f32[1024]{0:T(1024)} %param.21) | copy-start | bytes 12292
  786.6 123.3 %copy-start.22 = (f32[512]{0:T(512)S(1)}, f32[512]{0:T(512)}, u32[]{:S(2)}) copy-start(f32[512]{0:T(512)} %copy-done.21) | copy-start | bytes 6148
  786.6 123.2 %copy-start.27 = (f32[512]{0:T(512)S(1)}, f32[512]{0:T(512)}, u32[]{:S(2)}) copy-start(f32[512]{0:T(512)} %copy-done.26) | copy-start | bytes 6148
  (16 other events, 31.4 us)
Sparse Core Ops, SparseCore 0:
  12.1 62.0 all-gather.4
  161.7 52.6 reduce-scatter.17
  219.5 52.6 all-gather.6
  274.0 52.6 all-gather.8
  347.3 52.6 reduce-scatter.21
  407.4 52.6 all-gather.10
  462.4 34.1 reduce-scatter.33
  498.9 32.3 reduce-scatter.31
  533.6 32.3 reduce-scatter.29
  734.3 31.0 reduce-scatter.27
  767.8 32.5 reduce-scatter.25
  803.5 50.3 reduce-scatter.23
  856.9 52.9 reduce-scatter.19
where the time goes:
time: 935 us; the launch traced here: 923 us
  waiting for transfers between devices  343 us (37%)
  matrix products  252 us (27%)
  local copies, waits for them, and re-layouts  125 us (13%)
  other arithmetic  121 us (13%)
  blocking collectives  39.8 us (4%)
  between operations  18.2 us (2%)
  loops' own time  14.5 us (2%)
  starting transfers between devices  9.52 us (1%)
    reduce_scatter x1, waiting for transfers between devices, shards(): lax.psum_scatter(jnp.dot(row_block_part, w_out, preferred_element_type=jn...  52.8 us
    reduce_scatter x1, waiting for transfers between devices, shards(): lax.psum_scatter((jnp.einsum('tf,df->td', d_gate, gate_full, preferred_el...  52.8 us
    all_gather x1, waiting for transfers between devices, shards(): ffn_input = lax.all_gather(second_normed_rows, 'tensor', axis=0, tiled=True)  52.2 us
    reduce_scatter x1, waiting for transfers between devices, shards(): lax.psum_scatter(jnp.einsum('te,ce->tc', row_block_part, w_qkv, preferred...  51.8 us
    dot_general x4, matrix products, back_block(): jnp.einsum('qhd,khd->hqk', grad_part, value_row, preferred_element_type=j...  51.4 us
    convert_element_type x4, other arithmetic, back_block(): d_scores = (probabilities * (d_prob - centre)).astype(jnp.bfloat16)  48.6 us
    dynamic_update_slice x8, local copies, waits for them, and re-layouts, attend_row(): block_outs, logsums = lax.map(attend_block, jnp.arange(block_count))  46.5 us
    all_gather x1, waiting for transfers between devices, shards(): out_rows = lax.all_gather(out_grad, 'tensor', axis=0, tiled=True)  41.1 us
  transfers between devices with their start and end apart: 15, of which 10 were waited for; matrix products, arithmetic and copies ran while one was open for 37% of the time, Pallas kernels for 0%

commit v1 on v0

v1 whole, which is shorter than its diff:
```python
import functools
import math

import jax
import jax.numpy as jnp
import numpy as np
from jax import lax
from jax.experimental import pallas as pl
from jax.experimental.pallas import tpu as pltpu
from jax.sharding import PartitionSpec as P

HD = 64
HALF = HD // 2
LANES = 128
GROUP = LANES // HALF
EPS = 1e-06
NEG = -1e30
f32 = jnp.float32
bf16 = jnp.bfloat16


def rope_tables(length):
    inverse = jnp.exp(-math.log(10000.0) * jnp.arange(HALF, dtype=f32) / HALF)
    angles = jnp.arange(length, dtype=f32)[:, None] * inverse[None, :]
    tile = lambda t: jnp.concatenate([t] * GROUP, axis=1)
    return tile(jnp.cos(angles)), tile(jnp.sin(angles))


def column_order(heads):
    value_width = max(LANES, heads * HD)
    order = np.full((4 * LANES + value_width,), -1, np.int32)
    for h in range(heads):
        for part in range(2):
            for half in range(2):
                at = (2 * part + half) * LANES + h * HALF
                src = h * 3 * HD + part * HD + half * HALF
                order[at : at + HALF] = np.arange(src, src + HALF)
        order[4 * LANES + h * HD : 4 * LANES + (h + 1) * HD] = np.arange(
            h * 3 * HD + 2 * HD, (h + 1) * 3 * HD
        )
    return order


def column_selector(heads):
    order = jnp.asarray(column_order(heads))
    rows = jnp.arange(3 * heads * HD, dtype=jnp.int32)
    return (rows[:, None] == order[None, :]).astype(bf16)


def dot_nt(a, b):
    return lax.dot_general(a, b, (((1,), (1,)), ((), ())), preferred_element_type=f32)


def dot_tn(a, b):
    return lax.dot_general(a, b, (((0,), (0,)), ((), ())), preferred_element_type=f32)


def dot_nn(a, b):
    return jnp.dot(a, b, preferred_element_type=f32)


def project_kernel(
    heads, x_ref, w_ref, fv_ref, cos_ref, sin_ref, lim_ref, q_ref, k_ref, v_ref, sq_ref
):
    rows = x_ref.shape[0]
    at = pl.program_id(0)
    acc = dot_nn(x_ref[...], w_ref[...])
    c, s = cos_ref[...], sin_ref[...]
    lane = lax.broadcasted_iota(jnp.int32, (rows, LANES), 1)
    place = at * rows + lax.broadcasted_iota(jnp.int32, (rows, LANES), 0)
    inside = (place >= lim_ref[0:1, :]) & (place < lim_ref[1:2, :])
    doc_lane = (lane >= HD) & (lane < HD + 8)
    q_extra = jnp.where(doc_lane & jnp.logical_not(inside), NEG, 0.0)
    k_extra = jnp.where(inside, 1.0, jnp.where((lane >= HD + 8) & (lane < HD + 11), 1.0, 0.0))
    for ref, base, extra, scale in ((q_ref, 0, q_extra, HD**-0.5), (k_ref, 2, k_extra, 1.0)):
        u1 = acc[:, base * LANES : (base + 1) * LANES]
        u2 = acc[:, (base + 1) * LANES : (base + 2) * LANES]
        r1 = (u1 * c - u2 * s) * scale
        r2 = (u1 * s + u2 * c) * scale
        for h in range(heads):
            a = r1 if h == 0 else pltpu.roll(r1, LANES - HALF * h, 1)
            b = r2 if h == 1 else pltpu.roll(r2, (LANES + HALF - HALF * h) % LANES, 1)
            both = jnp.where(lane < HALF, a, jnp.where(lane < HD, b, extra))
            ref[:, h * LANES : (h + 1) * LANES] = both.astype(bf16)

    @pl.when(at == 0)
    def _():
        sq_ref[...] = jnp.zeros_like(sq_ref)

    width = fv_ref.shape[1]
    first = fv_ref[...].astype(f32)
    mixed = 0.5 * acc[:, 4 * LANES :] + 0.5 * first
    sq_ref[0:1, :] += jnp.sum(mixed * mixed, axis=0, keepdims=True)
    sq_ref[1:2, :] += jnp.sum(first * first, axis=0, keepdims=True)
    for h in range(heads):
        t = (h // 2) * LANES
        own = (lane < HD) if h % 2 == 0 else (lane >= HD)
        v_ref[:, h * LANES : (h + 1) * LANES] = jnp.where(
            own, mixed[:, t : t + LANES], 1.0
        ).astype(bf16)


def project(heads, x, w, fv, cos, sin, limits, rows=512):
    length = x.shape[0]
    width = fv.shape[1]
    row = lambda i: (i, 0)
    whole = lambda i: (0, 0)
    ext = heads * LANES
    return pl.pallas_call(
        functools.partial(project_kernel, heads),
        name="project",
        grid=(length // rows,),
        in_specs=[
            pl.BlockSpec((rows, x.shape[1]), row),
            pl.BlockSpec(w.shape, whole),
            pl.BlockSpec((rows, width), row),
            pl.BlockSpec((rows, LANES), row),
            pl.BlockSpec((rows, LANES), row),
            pl.BlockSpec((8, LANES), whole),
        ],
        out_specs=[
            pl.BlockSpec((rows, ext), row),
            pl.BlockSpec((rows, ext), row),
            pl.BlockSpec((rows, ext), row),
            pl.BlockSpec((8, width), whole),
        ],
        out_shape=[
            jax.ShapeDtypeStruct((length, ext), bf16),
            jax.ShapeDtypeStruct((length, ext), bf16),
            jax.ShapeDtypeStruct((length, ext), bf16),
            jax.ShapeDtypeStruct((8, width), f32),
        ],
        compiler_params=pltpu.CompilerParams(vmem_limit_bytes=40 << 20),
        cost_estimate=pl.CostEstimate(
            flops=2 * length * x.shape[1] * w.shape[1],
            bytes_accessed=2 * (x.size + w.size + fv.size + 3 * length * ext),
            transcendentals=0,
        ),
    )(x, w, fv, cos, sin, limits)


def pieces(x):
    hi = x.astype(bf16).astype(f32)
    mid = (x - hi).astype(bf16).astype(f32)
    return hi, mid, x - hi - mid


def attend_kernel(heads, block, begin_ref, q_ref, k_ref, v_ref, o_ref, qo_ref, m_ref, acc_ref):
    at = pl.program_id(0)
    lane = lax.broadcasted_iota(jnp.int32, (block, LANES), 1)
    r = lax.broadcasted_iota(jnp.int32, (block, block), 0)
    c = lax.broadcasted_iota(jnp.int32, (block, block), 1)
    causal = c <= r
    here = pl.ds(pl.multiple_of(at * block, block), block)
    col = [slice(h * LANES, (h + 1) * LANES) for h in range(heads)]
    for h in range(heads):
        s = dot_nt(q_ref[:, col[h]], k_ref[here, col[h]])
        s = jnp.where(causal, s, NEG)
        m = jnp.max(s, axis=1, keepdims=True)
        p = jnp.exp(s - m).astype(bf16)
        m_ref[:, col[h]] = jnp.broadcast_to(m, (block, LANES))
        acc_ref[:, col[h]] = dot_nn(p, v_ref[here, col[h]])

    def step(kb, carry):
        there = pl.ds(pl.multiple_of(kb * block, block), block)
        for h in range(heads):
            s = dot_nt(q_ref[:, col[h]], k_ref[there, col[h]])
            old = m_ref[:, col[h]]
            new = jnp.maximum(old, jnp.max(s, axis=1, keepdims=True))
            p = jnp.exp(s - jnp.concatenate([new] * (block // LANES), axis=1)).astype(bf16)
            m_ref[:, col[h]] = new
            acc_ref[:, col[h]] = acc_ref[:, col[h]] * jnp.exp(old - new) + dot_nn(
                p, v_ref[there, col[h]]
            )
        return carry

    lax.fori_loop(begin_ref[at], at, step, 0)
    low = lane < HD
    for t in range((heads + 1) // 2):
        a = acc_ref[:, col[2 * t]]
        b = acc_ref[:, col[2 * t + 1]] if 2 * t + 1 < heads else a
        total = pltpu.roll(jnp.where(low, b, a), HD, 1)
        o_ref[:, t * LANES : (t + 1) * LANES] = (jnp.where(low, a, b) / total).astype(bf16)
    for h in range(heads):
        a = acc_ref[:, col[h]]
        total = a if h % 2 == 0 else pltpu.roll(a, HD, 1)
        hi, mid, lo = pieces(-(m_ref[:, col[h]] + jnp.log(jnp.where(low, 1.0, total))))
        extra = jnp.where(
            lane == HD + 8, hi, jnp.where(lane == HD + 9, mid, jnp.where(lane == HD + 10, lo, 0.0))
        )
        fill = (lane >= HD + 8) & (lane < HD + 11)
        qo_ref[:, col[h]] = jnp.where(fill, extra, q_ref[:, col[h]].astype(f32)).astype(bf16)


def attend(heads, q, k, v, begins, block):
    length = q.shape[0]
    ext = heads * LANES
    width = max(LANES, heads * HD)
    row = lambda i, b: (i, 0)
    whole = lambda i, b: (0, 0)
    return pl.pallas_call(
        functools.partial(attend_kernel, heads, block),
        name="attend",
        grid_spec=pltpu.PrefetchScalarGridSpec(
            num_scalar_prefetch=1,
            grid=(length // block,),
            in_specs=[
                pl.BlockSpec((block, ext), row),
                pl.BlockSpec((length, ext), whole),
                pl.BlockSpec((length, ext), whole),
            ],
            out_specs=[pl.BlockSpec((block, width), row), pl.BlockSpec((block, ext), row)],
            scratch_shapes=[pltpu.VMEM((block, ext), f32), pltpu.VMEM((block, ext), f32)],
        ),
        out_shape=[
            jax.ShapeDtypeStruct((length, width), bf16),
            jax.ShapeDtypeStruct((length, ext), bf16),
        ],
        compiler_params=pltpu.CompilerParams(vmem_limit_bytes=40 << 20),
        cost_estimate=pl.CostEstimate(
            flops=2 * heads * length * length * LANES,
            bytes_accessed=2 * 5 * length * ext,
            transcendentals=heads * length * length // 2,
        ),
    )(begins, q, k, v)


def attend_back_kernel(
    heads, block, begin_ref, q_ref, k_ref, v_ref, do_ref, o_ref, cos_ref, sin_ref, g_ref,
    dk_ref, dv_ref, dq_ref, de_ref,
):
    at = pl.program_id(0)
    lane = lax.broadcasted_iota(jnp.int32, (block, LANES), 1)
    r = lax.broadcasted_iota(jnp.int32, (block, block), 0)
    c = lax.broadcasted_iota(jnp.int32, (block, block), 1)
    causal = r <= c
    low = lane < HD
    here = pl.ds(pl.multiple_of(at * block, block), block)
    col = [slice(h * LANES, (h + 1) * LANES) for h in range(heads)]

    for h in range(heads):
        t = slice((h // 2) * LANES, (h // 2 + 1) * LANES)
        own = low if h % 2 == 0 else jnp.logical_not(low)
        grad = do_ref[:, t].astype(f32)
        centre = jnp.sum(jnp.where(own, grad * o_ref[:, t].astype(f32), 0.0), axis=1, keepdims=True)
        hi, mid, lo = pieces(-jnp.broadcast_to(centre, (block, LANES)))
        spot = lane - (HD if h % 2 == 0 else 0)
        extra = jnp.where(spot == 0, hi, jnp.where(spot == 1, mid, jnp.where(spot == 2, lo, 0.0)))
        de_ref[:, col[h]] = jnp.where(own, grad, extra).astype(bf16)

    def pair(there, h, mask, first):
        st = dot_nt(k_ref[there, col[h]], q_ref[:, col[h]])
        p = jnp.exp(st)
        if mask is not None:
            p = jnp.where(mask, p, 0.0)
        dpt = dot_nt(v_ref[there, col[h]], de_ref[:, col[h]])
        ds = (p * dpt).astype(bf16)
        dv = dot_nn(p.astype(bf16), de_ref[:, col[h]])
        dk = dot_nn(ds, q_ref[:, col[h]])
        dq = dot_tn(ds, k_ref[there, col[h]])
        if first:
            dv_ref[there, col[h]] = dv
            dk_ref[there, col[h]] = dk
            dq_ref[:, col[h]] = dq
        else:
            dv_ref[there, col[h]] += dv
            dk_ref[there, col[h]] += dk
            dq_ref[:, col[h]] += dq

    for h in range(heads):
        pair(here, h, causal, True)

    def step(kb, carry):
        there = pl.ds(pl.multiple_of(kb * block, block), block)
        for h in range(heads):
            pair(there, h, None, False)
        return carry

    lax.fori_loop(begin_ref[at], at, step, 0)

    def turn_back(ref, rows, base, scale):
        u1 = u2 = None
        quarter = lane // HALF
        for h in range(heads):
            u = ref[rows, col[h]]
            a = u if h == 0 else pltpu.roll(u, HALF * h, 1)
            b = u if h == 1 else pltpu.roll(u, (LANES + HALF * h - HALF) % LANES, 1)
            u1 = a if h == 0 else jnp.where(quarter == h, a, u1)
            u2 = b if h == 0 else jnp.where(quarter == h, b, u2)
        if heads < GROUP:
            u1 = jnp.where(quarter < heads, u1, 0.0)
            u2 = jnp.where(quarter < heads, u2, 0.0)
        u1, u2 = u1 * scale, u2 * scale
        cs, sn = cos_ref[rows, :], sin_ref[rows, :]
        return (u1 * cs + u2 * sn).astype(bf16), (u2 * cs - u1 * sn).astype(bf16)

    def finish(i, carry):
        rows = pl.ds(pl.multiple_of(i * block, block), block)
        d1, d2 = turn_back(dk_ref, rows, 2, 1.0)
        g_ref[rows, 2 * LANES : 3 * LANES] = d1
        g_ref[rows, 3 * LANES : 4 * LANES] = d2
        for t in range((heads + 1) // 2):
            a = dv_ref[rows, col[2 * t]]
            b = dv_ref[rows, col[2 * t + 1]] if 2 * t + 1 < heads else jnp.zeros_like(a)
            d_mix = jnp.where(low, a, b).astype(bf16)
            g_ref[rows, (4 + t) * LANES : (5 + t) * LANES] = (d_mix.astype(f32) * 0.5).astype(bf16)
        return carry

    u1 = u2 = None
    quarter = lane // HALF
    for h in range(heads):
        u = dq_ref[:, col[h]]
        a = u if h == 0 else pltpu.roll(u, HALF * h, 1)
        b = u if h == 1 else pltpu.roll(u, (LANES + HALF * h - HALF) % LANES, 1)
        u1 = a if h == 0 else jnp.where(quarter == h, a, u1)
        u2 = b if h == 0 else jnp.where(quarter == h, b, u2)
    if heads < GROUP:
        u1 = jnp.where(quarter < heads, u1, 0.0)
        u2 = jnp.where(quarter < heads, u2, 0.0)
    u1, u2 = u1 * HD**-0.5, u2 * HD**-0.5
    cs, sn = cos_ref[here, :], sin_ref[here, :]
    g_ref[here, 0:LANES] = (u1 * cs + u2 * sn).astype(bf16)
    g_ref[here, LANES : 2 * LANES] = (u2 * cs - u1 * sn).astype(bf16)

    @pl.when(at == pl.num_programs(0) - 1)
    def _():
        lax.fori_loop(0, pl.num_programs(0), finish, 0)


def attend_back(heads, q, k, v, d_out, out, cos, sin, begins, block):
    length = q.shape[0]
    ext = heads * LANES
    width = out.shape[1]
    row = lambda i, b: (i, 0)
    whole = lambda i, b: (0, 0)
    return pl.pallas_call(
        functools.partial(attend_back_kernel, heads, block),
        name="attend_back",
        grid_spec=pltpu.PrefetchScalarGridSpec(
            num_scalar_prefetch=1,
            grid=(length // block,),
            in_specs=[
                pl.BlockSpec((block, ext), row),
                pl.BlockSpec((length, ext), whole),
                pl.BlockSpec((length, ext), whole),
                pl.BlockSpec((block, width), row),
                pl.BlockSpec((block, width), row),
                pl.BlockSpec((length, LANES), whole),
                pl.BlockSpec((length, LANES), whole),
            ],
            out_specs=pl.BlockSpec((length, 4 * LANES + width), whole),
            scratch_shapes=[
                pltpu.VMEM((length, ext), f32),
                pltpu.VMEM((length, ext), f32),
                pltpu.VMEM((block, ext), f32),
                pltpu.VMEM((block, ext), bf16),
            ],
        ),
        out_shape=jax.ShapeDtypeStruct((length, 4 * LANES + width), bf16),
        compiler_params=pltpu.CompilerParams(vmem_limit_bytes=48 << 20),
        cost_estimate=pl.CostEstimate(
            flops=5 * heads * length * length * LANES,
            bytes_accessed=2 * 8 * length * ext,
            transcendentals=heads * length * length // 2,
        ),
    )(begins, q, k, v, d_out, out, cos, sin)


def rms_normalize(row_block):
    inverse = lax.rsqrt(jnp.mean(row_block * row_block, axis=-1, keepdims=True) + EPS)
    return (row_block * inverse, inverse)


def rms_normalize_backward(normed, inverse, gain_vec, incoming):
    scaled = incoming * gain_vec
    inner_mean = jnp.mean(scaled * normed, axis=-1, keepdims=True)
    return (inverse * (scaled - normed * inner_mean), jnp.sum(incoming * normed, axis=0))


def shards(
    tokens,
    first_values,
    doc_lengths,
    attention_norm_gain,
    w_qkv,
    w_out,
    feedforward_norm_gain,
    w_gate,
    w_up,
    w_down,
    out_grad,
):
    local_rows = tokens.shape[0]
    heads = w_out.shape[0] // HD
    width = max(LANES, heads * HD)
    length = local_rows * lax.axis_size("tensor")
    block = 256
    cosine, sine_table = rope_tables(length)
    ends = jnp.cumsum(doc_lengths[0])
    starts = ends - doc_lengths[0]
    limits = jnp.zeros((8, LANES), jnp.int32)
    docs = doc_lengths.shape[1]
    limits = limits.at[0, HD : HD + docs].set(starts).at[1, HD : HD + docs].set(ends)
    heads_at = jnp.arange(length // block, dtype=jnp.int32) * block
    begins = jnp.max(jnp.where(starts[None, :] <= heads_at[:, None], starts[None, :], 0), axis=1)
    begins = (begins // block).astype(jnp.int32)
    select = column_selector(heads)
    w_cols = jnp.dot(w_qkv, select, preferred_element_type=f32).astype(bf16)

    residual_input = tokens.astype(f32)
    first_unit_rows, first_inverse_rms = rms_normalize(residual_input)
    first_normed_rows = (first_unit_rows * attention_norm_gain).astype(bf16)
    normed_all = lax.all_gather(first_normed_rows, "tensor", axis=0, tiled=True)
    first_local = lax.all_to_all(first_values, "tensor", split_axis=1, concat_axis=0, tiled=True)
    if width > heads * HD:
        first_local = jnp.pad(first_local, ((0, 0), (0, width - heads * HD)))
    q, k, v, squares = project(
        heads, normed_all, w_cols, first_local, cosine, sine_table, limits
    )
    attended_wide, q = attend(heads, q, k, v, begins, block)
    attended = attended_wide[:, : heads * HD]
    middle_stream = residual_input + lax.psum_scatter(
        jnp.dot(attended, w_out, preferred_element_type=f32).astype(bf16),
        "tensor",
        scatter_dimension=0,
        tiled=True,
    ).astype(f32)
    second_unit_rows, second_inverse_rms = rms_normalize(middle_stream)
    second_normed_rows = (second_unit_rows * feedforward_norm_gain).astype(bf16)
    gate_full, up_full, down_full = (w_gate, w_up, w_down)
    ffn_input = lax.all_gather(second_normed_rows, "tensor", axis=0, tiled=True)
    gate_act = jnp.dot(ffn_input, gate_full, preferred_element_type=f32)
    up_act = jnp.dot(ffn_input, up_full, preferred_element_type=f32)
    sigmoid_gate = jax.nn.sigmoid(gate_act)
    hidden = (gate_act * sigmoid_gate * up_act).astype(bf16)
    ffn_out = lax.psum_scatter(
        jnp.dot(hidden, down_full, preferred_element_type=f32).astype(bf16),
        "tensor",
        scatter_dimension=0,
        tiled=True,
    ).astype(f32)
    out = (middle_stream + ffn_out).astype(bf16)
    out_rows = lax.all_gather(out_grad, "tensor", axis=0, tiled=True)
    down_grad = jnp.einsum("tf,td->fd", hidden, out_rows, preferred_element_type=f32)
    d_hidden = jnp.einsum("td,fd->tf", out_rows, down_full, preferred_element_type=f32)
    d_up = (d_hidden * gate_act * sigmoid_gate).astype(bf16)
    d_gate = (d_hidden * up_act * sigmoid_gate * (1.0 + gate_act * (1.0 - sigmoid_gate))).astype(
        bf16
    )
    gate_grad = jnp.einsum("td,tf->df", ffn_input, d_gate, preferred_element_type=f32)
    up_grad = jnp.einsum("td,tf->df", ffn_input, d_up, preferred_element_type=f32)
    second_normed_cotangent = lax.psum_scatter(
        (
            jnp.einsum("tf,df->td", d_gate, gate_full, preferred_element_type=f32)
            + jnp.einsum("tf,df->td", d_up, up_full, preferred_element_type=f32)
        ).astype(bf16),
        "tensor",
        scatter_dimension=0,
        tiled=True,
    ).astype(f32)
    middle_norm_cotangent, feedforward_gain_share = rms_normalize_backward(
        second_unit_rows, second_inverse_rms, feedforward_norm_gain, second_normed_cotangent
    )
    d_middle = out_grad.astype(f32) + middle_norm_cotangent
    d_branch = lax.all_gather(d_middle.astype(bf16), "tensor", axis=0, tiled=True)
    out_weight_grad = jnp.einsum("te,td->ed", attended, d_branch, preferred_element_type=f32)
    d_attended = jnp.einsum("td,ed->te", d_branch, w_out, preferred_element_type=f32).astype(bf16)
    if width > heads * HD:
        d_attended = jnp.pad(d_attended, ((0, 0), (0, width - heads * HD)))
    d_qkv = attend_back(
        heads, q, k, v, d_attended, attended_wide, cosine, sine_table, begins, block
    )
    d_half = d_qkv[:, 4 * LANES : 4 * LANES + heads * HD]
    qkv_grad = jnp.einsum("tc,te->ce", normed_all, d_qkv, preferred_element_type=f32).astype(bf16)
    qkv_grad = jnp.einsum("ce,fe->cf", qkv_grad, select, preferred_element_type=f32)
    first_normed_cotangent = lax.psum_scatter(
        jnp.einsum("te,ce->tc", d_qkv, w_cols, preferred_element_type=f32).astype(bf16),
        "tensor",
        scatter_dimension=0,
        tiled=True,
    ).astype(f32)
    first_grad = lax.all_to_all(
        d_half, "tensor", split_axis=0, concat_axis=1, tiled=True
    ).astype(f32)
    input_norm_cotangent, attention_gain_share = rms_normalize_backward(
        first_unit_rows, first_inverse_rms, attention_norm_gain, first_normed_cotangent
    )
    tokens_grad = d_middle + input_norm_cotangent
    scatter = lambda g, dim: lax.psum_scatter(
        g.astype(bf16), "dp", scatter_dimension=dim, tiled=True
    ).astype(f32)
    reduced = (
        scatter(qkv_grad, 0),
        scatter(out_weight_grad, 1),
        scatter(gate_grad, 0),
        scatter(up_grad, 0),
        scatter(down_grad, 1),
    )
    attn_gain_grad, ffn_gain_grad, mixed_total, first_total = lax.psum(
        (attention_gain_share, feedforward_gain_share, jnp.sum(squares[0]), jnp.sum(squares[1])),
        ("dp", "tensor"),
    )
    entry_count = first_values.size * lax.axis_size("dp") * lax.axis_size("tensor")
    return (
        out,
        tokens_grad,
        first_grad,
        attn_gain_grad,
        reduced[0],
        reduced[1],
        ffn_gain_grad,
        reduced[2],
        reduced[3],
        reduced[4],
        jnp.sqrt(first_total / entry_count),
        jnp.sqrt(mixed_total / entry_count),
    )


def solution(mesh):
    token_spec = P(("dp", "tensor"), None)
    return jax.shard_map(
        shards,
        mesh=mesh,
        in_specs=(
            token_spec,
            token_spec,
            P("dp", None),
            P(),
            P(None, "tensor"),
            P("tensor", None),
            P(),
            P(None, "tensor"),
            P(None, "tensor"),
            P("tensor", None),
            token_spec,
        ),
        out_specs=(
            token_spec,
            token_spec,
            token_spec,
            P(),
            P("dp", "tensor"),
            P("tensor", "dp"),
            P(),
            P("dp", "tensor"),
            P("dp", "tensor"),
            P("tensor", "dp"),
            P(),
            P(),
        ),
        check_vma=False,
    )
```

time: 935 us -> 712 us (0.76)
  matrix products: 252 us -> 91 us
  local copies, waits for them, and re-layouts: 125 us -> 23.9 us
  other arithmetic: 121 us -> 34 us
  waiting for transfers between devices: 343 us -> 417 us
  Pallas kernels: 0 us -> 69 us
  loops' own time: 14.5 us -> 0 us
    dot_general x43 -> x15, matrix products: 252 us -> 91 us  [the longest x1 11.8 us: shards(): jnp.einsum('td,fd->tf', out_rows, down_full, preferred_element_type=f32)]
    pallas_call x0 -> x3, Pallas kernels: none -> 69 us  [the longest x1 39.8 us: attend_back(): pl.pallas_call(functools.partial(attend_back_kernel, heads, block), name=...]
    convert_element_type x16 -> x8, other arithmetic: 66.7 us -> 11.9 us  [the longest x5 4.68 us: shards(): scatter = lambda g, dim: lax.psum_scatter(g.astype(bf16), 'dp', scatter_d...]
    unnamed x17, waiting for transfers between devices: 0.73 us -> 48.9 us
    dynamic_update_slice x8 -> x0, local copies, waits for them, and re-layouts: 46.5 us -> none  [attend_row(): block_outs, logsums = lax.map(attend_block, jnp.arange(block_count))]
    while x32 -> x0, local copies, waits for them, and re-layouts: 26.7 us -> none
    reduce_scatter x4, waiting for transfers between devices: 126 us -> 151 us  [the longest x1 52.8 us: shards(): lax.psum_scatter(jnp.dot(attended, w_out, preferred_element_type=f32).ast...]
    reduce_sum x7 -> x1, other arithmetic: 23.2 us -> 0.6 us  [shards(): jnp.sum(squares[0])]
  transfers between devices with their start and end apart: 15 -> 15, of which waited for: 10 -> 12; matrix products, arithmetic and copies ran while one was open for 37% -> 14% of each run, Pallas kernels for 0% -> 6%
where the time goes in v1:
time: 712 us; the launch traced here: 703 us
  waiting for transfers between devices  417 us (59%)
  matrix products  91 us (13%)
  Pallas kernels  69 us (10%)
  blocking collectives  39.8 us (6%)
  other arithmetic  34 us (5%)
  local copies, waits for them, and re-layouts  23.9 us (3%)
  between operations  18.4 us (3%)
  starting transfers between devices  9.81 us (1%)
    reduce_scatter x1, waiting for transfers between devices, shards(): lax.psum_scatter((jnp.einsum('tf,df->td', d_gate, gate_full, preferred_el...  52.8 us
    reduce_scatter x1, waiting for transfers between devices, shards(): lax.psum_scatter(jnp.dot(attended, w_out, preferred_element_type=f32).ast...  52.8 us
    all_gather x1, waiting for transfers between devices, shards(): ffn_input = lax.all_gather(second_normed_rows, 'tensor', axis=0, tiled=True)  52.2 us
    reduce_scatter x1, waiting for transfers between devices, shards(): lax.psum_scatter(jnp.einsum('te,ce->tc', d_qkv, w_cols, preferred_element...  52 us
    unnamed x17, waiting for transfers between devices  48.9 us
    all_gather x1, waiting for transfers between devices, shards(): out_rows = lax.all_gather(out_grad, 'tensor', axis=0, tiled=True)  41 us
    pallas_call x1, Pallas kernels, attend_back(): pl.pallas_call(functools.partial(attend_back_kernel, heads, block), name=...  39.8 us
    psum x1, blocking collectives, shards(): lax.psum((attention_gain_share, feedforward_gain_share, jnp.sum(squares[0...  39.8 us
  transfers between devices with their start and end apart: 15, of which 12 were waited for; matrix products, arithmetic and copies ran while one was open for 14% of the time, Pallas kernels for 6%

profile of v1, /device:TPU:0, one launch (start us, length us, event | category | flops | bytes accessed | tf_op | source)
XLA Modules:
  0.0 702.7 jit_solution(15300157200110948798)
XLA Ops:
  7.2 1.7 fusion.18
  8.9 2.5 fusion.15
  12.5 5.2 all-to-all-start
  19.8 1.6 scatter.6
  21.8 3.9 fusion.24
  25.7 3.0 pad_maximum_fusion
  28.7 2.6 fusion.20
  31.3 7.8 %all-to-all-done = bf16[512,4,256]{2,0,1:T(8,128)(2,1)S(1)} async-done(((bf16[512,4,256]{2,0,1:T(8,128)(2,1)}), bf16[512,4,256]{2,0,1:T(8,128)(2,1)S(1)}, u32[]{:S(2)}, u32[]{:S(2)}) %all-to-all-start) | async-done | bytes 1048608 | tf_op jit(solution)/shard_map/all_to_all | solution.py:414
  39.1 34.2 %all-gather.5.cloned.1.call-done.x_ref = bf16[2048,1024]{1,0:T(8,128)(2,1)} async-done(((bf16[512,1024]{1,0:T(8,128)(2,1)}), bf16[2048,1024]{1,0:T(8,128)(2,1)}) %all-gather.5.cloned.1.call-update) | async-done | bytes 4194320 | tf_op jit(solution)/shard_map/all_gather | solution.py:413
  77.2 7.1 %project.1 = (bf16[2048,512]{1,0:T(8,128)(2,1)S(1)}, bf16[2048,512]{1,0:T(8,128)(2,1)S(1)}, bf16[2048,512]{1,0:T(8,128)(2,1)S(1)}, f32[8,256]{1,0:T(8,128)S(1)}) custom-call(bf16[2048,1024]{1,0:T(8,128)(2,1)} %all-gather.5.cloned.1.call-done.x_ref, bf16[1024,768]{1,0:T(8,128)(2,1)S(1)} %bitcast.53, bf16[2048,256]{1,0:T(8,128)(2,1)S(1)} %bitcast.52, ...), custom_call_target="tpu_custom_call" | custom-call | flops 3221225472 | bytes 13107200 | tf_op jit(solution)/shard_map/project/pallas_call | solution.py:109
  84.4 22.1 %attend.1 = (bf16[2048,256]{1,0:T(8,128)(2,1)S(1)}, bf16[2048,512]{1,0:T(8,128)(2,1)S(1)}) custom-call(s32[8]{0:T(128)S(1)} %and_select_fusion.begin_ref, bf16[2048,512]{1,0:T(8,128)(2,1)S(1)} %get-tuple-element.42.q_ref, bf16[2048,512]{1,0:T(8,128)(2,1)S(1)} %get-tuple-element.43.k_ref, bf16[2048,512]{1,0:T(8,128)(2,1)S(1)} %get-tuple-element.44.v_ref), custom_call_target="tpu_custom_call" | custom-call | flops 4294967296 | bytes 10485760 | tf_op jit(solution)/shard_map/attend/pallas_call | solution.py:201
  107.8 3.2 convolution_convert_fusion.1
  111.1 52.8 %reduce-scatter.18.cloned.1.call-done = bf16[512,1024]{1,0:T(8,128)(2,1)} async-done(((bf16[2048,1024]{1,0:T(8,128)(2,1)}), bf16[512,1024]{1,0:T(8,128)(2,1)}) %reduce-scatter.18.cloned.1.call-update) | async-done | bytes 1048592 | tf_op jit(solution)/shard_map/reduce_scatter | solution.py:422
  163.9 1.8 multiply_reduce_fusion
  167.7 52.2 %all-gather.7.cloned.1.call-done = bf16[2048,1024]{1,0:T(8,128)(2,1)} async-done(((bf16[512,1024]{1,0:T(8,128)(2,1)}), bf16[2048,1024]{1,0:T(8,128)(2,1)}) %all-gather.7.cloned.1.call-update) | async-done | bytes 4194320 | tf_op jit(solution)/shard_map/all_gather | solution.py:431
  219.9 8.5 %fusion.29 = f32[2048,704]{0,1:T(8,128)} fusion(bf16[2048,1024]{1,0:T(8,128)(2,1)} %all-gather.7.cloned.1.call-done, bf16[1024,704]{0,1:T(8,128)(2,1)} %param.24), kind=kOutput, calls=%fused_computation.75 | convolution fusion | flops 2952790016 | bytes 11403264 | tf_op jit(solution)/shard_map/dot_general | solution.py:433
  228.4 5.1 fusion.28
  233.5 41.0 %all-gather.9.cloned.1.call-done = bf16[2048,1024]{1,0:T(8,128)(2,1)} async-done(((bf16[512,1024]{1,0:T(8,128)(2,1)}), bf16[2048,1024]{1,0:T(8,128)(2,1)}) %all-gather.9.cloned.1.call-update) | async-done | bytes 4194320 | tf_op jit(solution)/shard_map/all_gather | solution.py:443
  274.5 11.8 %multiply_convert_fusion = (bf16[2048,704]{0,1:T(8,128)(2,1)S(1)}, bf16[2048,704]{0,1:T(8,128)(2,1)S(1)}, bf16[2048,704]{0,1:T(8,128)(2,1)}) fusion(f32[2048,704]{0,1:T(8,128)} %fusion.28, f32[2048,704]{0,1:T(8,128)} %fusion.29, bf16[2048,1024]{1,0:T(8,128)(2,1)} %all-gather.9.cloned.1.call-done, bf16[704,1024]{1,0:T(8,128)(2,1)} %param.25), kind=kOutput, calls=%fused_computation.1 | convolution fusion | flops 2975858688 | bytes 25821184 | tf_op jit(solution)/shard_map/td,fd->tf/dot_general | solution.py:445
  286.3 3.5 fusion.30
  289.9 5.1 add_convert_fusion
  295.0 52.8 %reduce-scatter.22.cloned.1.call-done = bf16[512,1024]{1,0:T(8,128)(2,1)} async-done(((bf16[2048,1024]{1,0:T(8,128)(2,1)}), bf16[512,1024]{1,0:T(8,128)(2,1)}) %reduce-scatter.22.cloned.1.call-update) | async-done | bytes 1048592 | tf_op jit(solution)/shard_map/reduce_scatter | solution.py:452
  347.8 2.6 fusion.14
  350.4 3.3 fusion.26
  354.0 6.2 convolution_convert_fusion.7
  360.2 1.6 copy.40
  361.9 6.6 convolution_convert_fusion.5
  368.4 1.6 copy.38
  370.1 6.2 convolution_convert_fusion.6
  378.2 28.5 %all-gather.11.cloned.1.call-done = bf16[2048,1024]{1,0:T(8,128)(2,1)} async-done(((bf16[512,1024]{1,0:T(8,128)(2,1)}), bf16[2048,1024]{1,0:T(8,128)(2,1)}) %all-gather.11.cloned.1.call-update) | async-done | bytes 4194320 | tf_op jit(solution)/shard_map/all_gather | solution.py:465
  406.6 3.5 convolution_convert_fusion.8
  411.1 3.6 convolution_convert_fusion.3.do_ref
  414.8 39.8 %attend_back.1 = bf16[2048,768]{1,0:T(8,128)(2,1)} custom-call(s32[8]{0:T(128)S(1)} %and_select_fusion.begin_ref, bf16[2048,512]{1,0:T(8,128)(2,1)} %copy-done.10, bf16[2048,512]{1,0:T(8,128)(2,1)} %copy-done.8, bf16[2048,512]{1,0:T(8,128)(2,1)} %copy-done.9, bf16[2048,256]{1,0:T(8,128)(2,1)S(1)} %convolution_convert_fusion.3.do_ref, ...), custom_call_target="tpu_custom_call" | custom-call | flops 10737418240 | bytes 16777216 | tf_op jit(solution)/shard_map/attend_back/pallas_call | solution.py:336
  454.7 11.2 %fusion.21 = bf16[1024,768]{1,0:T(8,128)(2,1)} fusion(s32[768]{0:T(1024)S(1)} %copy-done.28, bf16[2048,1024]{1,0:T(8,128)(2,1)} %all-gather.5.cloned.1.call-done.x_ref, bf16[2048,768]{1,0:T(8,128)(2,1)} %attend_back.1), kind=kOutput, calls=%fused_computation.41 | convolution fusion | flops 4431347712 | bytes 8915968 | tf_op jit(solution)/shard_map/ce,fe->cf/dot_general | solution.py:475
  466.2 7.0 convolution_convert_fusion.2
  474.6 7.0 convolution_convert_fusion
  481.6 2.3 slice.55
  483.9 3.5 all-to-all-start.1
  491.7 20.8 %reduce-scatter.30.cloned.1.call-done = bf16[128,704]{1,0:T(8,128)(2,1)} async-done(((bf16[1024,704]{1,0:T(8,128)(2,1)}), bf16[128,704]{1,0:T(8,128)(2,1)}) %reduce-scatter.30.cloned.1.call-update) | async-done | bytes 180240
  514.6 1.6 copy.43
  516.2 27.4 %reduce-scatter.28.cloned.1.call-done = bf16[128,256]{1,0:T(8,128)(2,1)} async-done(((bf16[1024,256]{1,0:T(8,128)(2,1)}), bf16[128,256]{1,0:T(8,128)(2,1)}) %reduce-scatter.28.cloned.1.call-update) | async-done | bytes 65552
  545.2 33.8 %reduce-scatter.26.cloned.1.call-done = bf16[128,768]{1,0:T(8,128)(2,1)} async-done(((bf16[1024,768]{1,0:T(8,128)(2,1)}), bf16[128,768]{1,0:T(8,128)(2,1)}) %reduce-scatter.26.cloned.1.call-update) | async-done | bytes 196624 | tf_op jit(solution)/shard_map/reduce_scatter | solution.py:489
  579.0 1.7 convert_element_type.127
  580.7 52.0 %reduce-scatter.24.cloned.1.call-done = bf16[512,1024]{1,0:T(8,128)(2,1)} async-done(((bf16[2048,1024]{1,0:T(8,128)(2,1)}), bf16[512,1024]{1,0:T(8,128)(2,1)}) %reduce-scatter.24.cloned.1.call-update) | async-done | bytes 1048592 | tf_op jit(solution)/shard_map/reduce_scatter | solution.py:476
  632.7 2.0 fusion.17
  634.8 39.8 %all-reduce = (f32[1024]{0:T(1024)}, f32[1024]{0:T(1024)}, f32[]{:T(128)}, f32[]{:T(128)}) all-reduce(f32[1024]{0:T(1024)S(1)} %get-tuple-element.50, f32[1024]{0:T(1024)S(1)} %get-tuple-element.48, f32[]{:T(128)} %get-tuple-element.53, f32[]{:T(128)} %get-tuple-element.52), channel_id=1, replica_groups=mesh['dp'=8,'tensor'=4] {'dp','tensor'}, use_global_device_ids=true, to_apply=%region_12.13 | all-reduce | flops 2050 | bytes 16400 | tf_op jit(solution)/shard_map/psum | solution.py:499
  676.0 12.7 %reduce-scatter.20.cloned.1.call-done = bf16[512,1024]{1,0:T(8,128)(2,1)} async-done(((bf16[2048,1024]{1,0:T(8,128)(2,1)}), bf16[512,1024]{1,0:T(8,128)(2,1)}) %reduce-scatter.20.cloned.1.call-update) | async-done | bytes 1048592 | tf_op jit(solution)/shard_map/reduce_scatter | solution.py:436
  688.7 4.7 fusion.10
  (122 shorter events, 24.0 us)
Async XLA Ops:
  7.2 21.5 %copy-start = (bf16[1024,768]{1,0:T(8,128)(2,1)S(1)}, bf16[1024,768]{1,0:T(8,128)(2,1)}, u32[]{:S(2)}) copy-start(bf16[1024,768]{1,0:T(8,128)(2,1)} %param.20) | copy-start | bytes 4718596
  7.2 4.3 copy-start.15
  7.2 66.2 %all-gather.5.cloned.1.call-start = ((), (), s32[]{:S(2)}) async-start(), calls=%async_computation.11 | async-start | bytes 5242880 | tf_op jit(solution)/shard_map/all_gather | solution.py:413
  11.5 6.2 copy-start.21
  11.5 7.0 copy-start.29
  12.5 26.6 %all-to-all-start = ((bf16[512,4,256]{2,0,1:T(8,128)(2,1)}), bf16[512,4,256]{2,0,1:T(8,128)(2,1)S(1)}, u32[]{:S(2)}, u32[]{:S(2)}) async-start(bf16[512,4,256]{2,0,1:T(8,128)(2,1)} %bitcast.55), calls=%async_computation | async-start | bytes 2097152 | tf_op jit(solution)/shard_map/all_to_all | solution.py:414
  17.7 146.2 %reduce-scatter.18.cloned.1.call-start = ((), (), s32[]{:S(2)}) async-start(), calls=%async_computation.12 | async-start | bytes 5242880 | tf_op jit(solution)/shard_map/reduce_scatter | solution.py:422
  25.7 3.0 copy-start.27
  73.4 1.2 copy-start.2
  74.6 1.2 copy-start.4
  75.8 1.4 copy-start.6
  84.3 22.1 %copy-start.8 = (bf16[2048,512]{1,0:T(8,128)(2,1)}, bf16[2048,512]{1,0:T(8,128)(2,1)S(1)}, u32[]{:S(2)}) copy-start(bf16[2048,512]{1,0:T(8,128)(2,1)S(1)} %get-tuple-element.43.k_ref) | copy-start | bytes 6291460
  84.3 22.1 %copy-start.9 = (bf16[2048,512]{1,0:T(8,128)(2,1)}, bf16[2048,512]{1,0:T(8,128)(2,1)S(1)}, u32[]{:S(2)}) copy-start(bf16[2048,512]{1,0:T(8,128)(2,1)S(1)} %get-tuple-element.44.v_ref) | copy-start | bytes 6291460
  84.3 23.5 %copy-start.16 = (bf16[256,1024]{1,0:T(8,128)(2,1)S(1)}, bf16[256,1024]{1,0:T(8,128)(2,1)}, u32[]{:S(2)}) copy-start(bf16[256,1024]{1,0:T(8,128)(2,1)} %param.21) | copy-start | bytes 1572868
  106.5 1.3 copy-start.10
  111.0 52.9 %copy-start.11 = (bf16[512,1024]{1,0:T(8,128)(2,1)S(1)}, bf16[512,1024]{1,0:T(8,128)(2,1)}, u32[]{:S(2)}) copy-start(bf16[512,1024]{1,0:T(8,128)(2,1)} %param.16) | copy-start | bytes 3145732
  111.0 54.6 %copy-start.17 = (f32[1024]{0:T(1024)S(1)}, f32[1024]{0:T(1024)}, u32[]{:S(2)}) copy-start(f32[1024]{0:T(1024)} %param.22) | copy-start | bytes 12292
  111.1 108.9 %all-gather.7.cloned.1.call-start = ((), (), s32[]{:S(2)}) async-start(), calls=%async_computation.13 | async-start | bytes 5242880 | tf_op jit(solution)/shard_map/all_gather | solution.py:431
  163.9 1.8 copy-start.13
  167.1 107.4 %all-gather.9.cloned.1.call-start = ((), (), s32[]{:S(2)}) async-start(), calls=%async_computation.15 | async-start | bytes 5242880 | tf_op jit(solution)/shard_map/all_gather | solution.py:443
  167.6 180.2 %reduce-scatter.22.cloned.1.call-start = ((), (), s32[]{:S(2)}) async-start(), calls=%async_computation.16 | async-start | bytes 5242880 | tf_op jit(solution)/shard_map/reduce_scatter | solution.py:452
  219.9 8.5 %copy-start.22 = (bf16[2048,1024]{1,0:T(8,128)(2,1)S(1)}, bf16[2048,1024]{1,0:T(8,128)(2,1)}, u32[]{:S(2)}) copy-start(bf16[2048,1024]{1,0:T(8,128)(2,1)} %all-gather.7.cloned.1.call-done) | copy-start | bytes 12582916
  219.9 8.5 %copy-start.23 = (bf16[1024,704]{0,1:T(8,128)(2,1)S(1)}, bf16[1024,704]{0,1:T(8,128)(2,1)}, u32[]{:S(2)}) copy-start(bf16[1024,704]{0,1:T(8,128)(2,1)} %param.23) | copy-start | bytes 4325380
  274.5 11.8 %copy-start.24 = (bf16[1024,704]{0,1:T(8,128)(2,1)S(1)}, bf16[1024,704]{0,1:T(8,128)(2,1)}, u32[]{:S(2)}) copy-start(bf16[1024,704]{0,1:T(8,128)(2,1)} %param.23) | copy-start | bytes 4325380
  286.3 3.5 copy-start.30
  286.3 3.5 copy-start.31
  286.3 3.5 copy-start.25
  294.9 111.7 %all-gather.11.cloned.1.call-start = ((), (), s32[]{:S(2)}) async-start(), calls=%async_computation.17 | async-start | bytes 5242880 | tf_op jit(solution)/shard_map/all_gather | solution.py:465
  347.8 2.6 copy-start.14
  350.4 3.4 copy-start.19
  353.8 134.2 %reduce-scatter.34.cloned.1.call-start = ((), (), s32[]{:S(2)}) async-start(), calls=%async_computation.23 | async-start | bytes 1769472
  361.8 128.0 %reduce-scatter.32.cloned.1.call-start = ((), (), s32[]{:S(2)}) async-start(), calls=%async_computation.22 | async-start | bytes 1769472
  370.1 142.5 %reduce-scatter.30.cloned.1.call-start = ((), (), s32[]{:S(2)}) async-start(), calls=%async_computation.21 | async-start | bytes 1769472
  377.9 165.6 %reduce-scatter.28.cloned.1.call-start = ((), (), s32[]{:S(2)}) async-start(), calls=%async_computation.20 | async-start | bytes 589824
  411.1 3.6 copy-start.3
  411.1 3.6 copy-start.5
  414.8 39.9 %copy-start.28 = (s32[768]{0:T(1024)S(1)}, s32[768]{0:T(1024)}, u32[]{:S(2)}) copy-start(s32[768]{0:T(1024)} %constant.98.clone) | copy-start | bytes 9220
  454.6 11.6 %copy-start.7 = (bf16[768,1024]{0,1:T(8,128)(2,1)S(1)}, bf16[768,1024]{0,1:T(8,128)(2,1)}, u32[]{:S(2)}) copy-start(bf16[768,1024]{0,1:T(8,128)(2,1)} %fusion.20) | copy-start | bytes 4718596
  454.7 124.4 %reduce-scatter.26.cloned.1.call-start = ((), (), s32[]{:S(2)}) async-start(), calls=%async_computation.19 | async-start | bytes 1769472 | tf_op jit(solution)/shard_map/reduce_scatter | solution.py:489
  465.9 166.8 %reduce-scatter.24.cloned.1.call-start = ((), (), s32[]{:S(2)}) async-start(), calls=%async_computation.18 | async-start | bytes 5242880 | tf_op jit(solution)/shard_map/reduce_scatter | solution.py:476
  473.2 1.4 copy-start.26
  473.3 215.4 %reduce-scatter.20.cloned.1.call-start = ((), (), s32[]{:S(2)}) async-start(), calls=%async_computation.14 | async-start | bytes 5242880 | tf_op jit(solution)/shard_map/reduce_scatter | solution.py:436
  483.9 30.5 %all-to-all-start.1 = ((bf16[4,512,256]{2,1,0:T(8,128)(2,1)}), bf16[4,512,256]{2,1,0:T(8,128)(2,1)S(1)}, u32[]{:S(2)}, u32[]{:S(2)}) async-start(bf16[4,512,256]{2,1,0:T(8,128)(2,1)} %bitcast.6), calls=%async_computation.5 | async-start | bytes 2097152 | tf_op jit(solution)/shard_map/all_to_all | solution.py:482
  514.6 118.1 %copy-start.12 = (bf16[512,1024]{1,0:T(8,128)(2,1)S(1)}, bf16[512,1024]{1,0:T(8,128)(2,1)}, u32[]{:S(2)}) copy-start(bf16[512,1024]{1,0:T(8,128)(2,1)} %param.16) | copy-start | bytes 3145732
  514.6 118.1 %copy-start.18 = (f32[1024]{0:T(1024)S(1)}, f32[1024]{0:T(1024)}, u32[]{:S(2)}) copy-start(f32[1024]{0:T(1024)} %param.19) | copy-start | bytes 12292
  516.2 172.5 %copy-start.20 = (f32[512]{0:T(512)S(1)}, f32[512]{0:T(512)}, u32[]{:S(2)}) copy-start(f32[512]{0:T(512)} %copy-done.19) | copy-start | bytes 6148
  688.7 4.7 copy-start.1
Sparse Core Ops, SparseCore 0:
  11.6 61.7 all-gather.4
  111.2 52.6 reduce-scatter.17
  167.2 52.6 all-gather.6
  221.8 52.6 all-gather.8
  295.1 52.6 reduce-scatter.21
  353.9 52.6 all-gather.10
  408.9 34.2 reduce-scatter.33
  445.6 32.1 reduce-scatter.31
  480.1 32.3 reduce-scatter.29
  514.7 28.8 reduce-scatter.27
  546.5 32.4 reduce-scatter.25
  582.1 50.5 reduce-scatter.23
  635.7 52.9 reduce-scatter.19

commit v2 on v1

v2 whole, which is shorter than its diff:
```python
import functools
import math

import jax
import jax.numpy as jnp
import numpy as np
from jax import lax
from jax.experimental import pallas as pl
from jax.experimental.pallas import tpu as pltpu
from jax.sharding import PartitionSpec as P

HD = 64
HALF = HD // 2
LANES = 128
GROUP = LANES // HALF
EPS = 1e-06
NEG = -1e30
VMEM = 60 << 20
f32 = jnp.float32
bf16 = jnp.bfloat16


def rope_tables(length):
    inverse = jnp.exp(-math.log(10000.0) * jnp.arange(HALF, dtype=f32) / HALF)
    angles = jnp.arange(length, dtype=f32)[:, None] * inverse[None, :]
    tile = lambda t: jnp.concatenate([t] * GROUP, axis=1)
    return tile(jnp.cos(angles)), tile(jnp.sin(angles))


def column_order(heads):
    value_width = max(LANES, heads * HD)
    order = np.full((4 * LANES + value_width,), -1, np.int32)
    for h in range(heads):
        for part in range(2):
            for half in range(2):
                at = (2 * part + half) * LANES + h * HALF
                src = h * 3 * HD + part * HD + half * HALF
                order[at : at + HALF] = np.arange(src, src + HALF)
        order[4 * LANES + h * HD : 4 * LANES + (h + 1) * HD] = np.arange(
            h * 3 * HD + 2 * HD, (h + 1) * 3 * HD
        )
    return order


def column_selector(heads):
    order = jnp.asarray(column_order(heads))
    rows = jnp.arange(3 * heads * HD, dtype=jnp.int32)
    return (rows[:, None] == order[None, :]).astype(bf16)


def dot_nt(a, b):
    return lax.dot_general(a, b, (((1,), (1,)), ((), ())), preferred_element_type=f32)


def dot_tn(a, b):
    return lax.dot_general(a, b, (((0,), (0,)), ((), ())), preferred_element_type=f32)


def dot_nn(a, b):
    return jnp.dot(a, b, preferred_element_type=f32)


def project_kernel(heads, n, rows, placed, info_ref, *refs):
    count = len(placed)
    pieces, values = refs[:count], refs[count : count + n]
    w_ref, cos_ref, sin_ref, lim_ref = refs[count + n : count + n + 4]
    q_ref, k_ref, v_ref, sq_ref, x_ref, fv_ref, sem = refs[count + n + 4 :]
    at = pl.program_id(0)
    block = q_ref.shape[0]

    @pl.when(at == 0)
    def _():
        sq_ref[...] = jnp.zeros_like(sq_ref)
        copies = []
        for i, (ref, (j, first)) in enumerate(zip(pieces, placed)):
            size = ref.shape[0]
            place = pl.multiple_of((info_ref[0] ^ j) * rows + first, size)
            copies.append(pltpu.make_async_copy(ref, x_ref.at[pl.ds(place, size)], sem.at[i]))
        for j, ref in enumerate(values):
            place = pl.multiple_of((info_ref[0] ^ j) * rows, rows)
            copies.append(
                pltpu.make_async_copy(ref, fv_ref.at[pl.ds(place, rows)], sem.at[count + j])
            )
        for copy in copies:
            copy.start()
        for copy in copies:
            copy.wait()

    here = pl.ds(pl.multiple_of(at * block, block), block)
    acc = dot_nn(x_ref[here, :], w_ref[...])
    c, s = cos_ref[...], sin_ref[...]
    lane = lax.broadcasted_iota(jnp.int32, (block, LANES), 1)
    place = at * block + lax.broadcasted_iota(jnp.int32, (block, LANES), 0)
    inside = (place >= lim_ref[0:1, :]) & (place < lim_ref[1:2, :])
    doc_lane = (lane >= HD) & (lane < HD + 8)
    q_extra = jnp.where(doc_lane & jnp.logical_not(inside), NEG, 0.0)
    k_extra = jnp.where(inside, 1.0, jnp.where((lane >= HD + 8) & (lane < HD + 11), 1.0, 0.0))
    for ref, base, extra, scale in ((q_ref, 0, q_extra, HD**-0.5), (k_ref, 2, k_extra, 1.0)):
        u1 = acc[:, base * LANES : (base + 1) * LANES]
        u2 = acc[:, (base + 1) * LANES : (base + 2) * LANES]
        r1 = (u1 * c - u2 * s) * scale
        r2 = (u1 * s + u2 * c) * scale
        for h in range(heads):
            a = r1 if h == 0 else pltpu.roll(r1, LANES - HALF * h, 1)
            b = r2 if h == 1 else pltpu.roll(r2, (LANES + HALF - HALF * h) % LANES, 1)
            both = jnp.where(lane < HALF, a, jnp.where(lane < HD, b, extra))
            ref[:, h * LANES : (h + 1) * LANES] = both.astype(bf16)

    first = fv_ref[here, :].astype(f32)
    mixed = 0.5 * acc[:, 4 * LANES :] + 0.5 * first
    sq_ref[0:1, :] += jnp.sum(mixed * mixed, axis=0, keepdims=True)
    sq_ref[1:2, :] += jnp.sum(first * first, axis=0, keepdims=True)
    for h in range(heads):
        t = (h // 2) * LANES
        own = (lane < HD) if h % 2 == 0 else (lane >= HD)
        v_ref[:, h * LANES : (h + 1) * LANES] = jnp.where(
            own, mixed[:, t : t + LANES], 1.0
        ).astype(bf16)


def project(heads, info, parts, values, w, cos, sin, limits, rows):
    n = len(values)
    length = rows * n
    depth = parts[0][0].shape[1]
    width = values[0].shape[1]
    block = min(length, 512)
    row = lambda i, info: (i, 0)
    whole = lambda i, info: (0, 0)
    ext = heads * LANES
    placed = tuple((j, first) for _, j, first in parts)
    anywhere = pl.BlockSpec(memory_space=pl.ANY)
    return pl.pallas_call(
        functools.partial(project_kernel, heads, n, rows, placed),
        name="project",
        grid_spec=pltpu.PrefetchScalarGridSpec(
            num_scalar_prefetch=1,
            grid=(length // block,),
            in_specs=[anywhere] * (len(parts) + n)
            + [
                pl.BlockSpec(w.shape, whole),
                pl.BlockSpec((block, LANES), row),
                pl.BlockSpec((block, LANES), row),
                pl.BlockSpec((8, LANES), whole),
            ],
            out_specs=[
                pl.BlockSpec((block, ext), row),
                pl.BlockSpec((block, ext), row),
                pl.BlockSpec((block, ext), row),
                pl.BlockSpec((8, width), whole),
                pl.BlockSpec((length, depth), whole),
            ],
            scratch_shapes=[
                pltpu.VMEM((length, width), bf16),
                pltpu.SemaphoreType.DMA((len(parts) + n,)),
            ],
        ),
        out_shape=[
            jax.ShapeDtypeStruct((length, ext), bf16),
            jax.ShapeDtypeStruct((length, ext), bf16),
            jax.ShapeDtypeStruct((length, ext), bf16),
            jax.ShapeDtypeStruct((8, width), f32),
            jax.ShapeDtypeStruct((length, depth), bf16),
        ],
        compiler_params=pltpu.CompilerParams(vmem_limit_bytes=VMEM),
        cost_estimate=pl.CostEstimate(
            flops=2 * length * depth * w.shape[1],
            bytes_accessed=2 * (2 * length * depth + w.size + length * width + 3 * length * ext),
            transcendentals=0,
        ),
    )(info, *[p for p, _, _ in parts], *values, w, cos, sin, limits)


def pieces(x):
    hi = x.astype(bf16).astype(f32)
    mid = (x - hi).astype(bf16).astype(f32)
    return hi, mid, x - hi - mid


def attend_kernel(
    heads, block, offset, steps, info_ref, begin_ref, q_ref, k_ref, v_ref, o_ref, qo_ref, m_ref,
    acc_ref,
):
    at = (info_ref[0] ^ offset) * steps + pl.program_id(0)
    lane = lax.broadcasted_iota(jnp.int32, (block, LANES), 1)
    r = lax.broadcasted_iota(jnp.int32, (block, block), 0)
    c = lax.broadcasted_iota(jnp.int32, (block, block), 1)
    causal = c <= r
    here = pl.ds(pl.multiple_of(at * block, block), block)
    col = [slice(h * LANES, (h + 1) * LANES) for h in range(heads)]
    for h in range(heads):
        s = dot_nt(q_ref[:, col[h]], k_ref[here, col[h]])
        s = jnp.where(causal, s, NEG)
        m = jnp.max(s, axis=1, keepdims=True)
        p = jnp.exp(s - m).astype(bf16)
        m_ref[:, col[h]] = jnp.broadcast_to(m, (block, LANES))
        acc_ref[:, col[h]] = dot_nn(p, v_ref[here, col[h]])

    def step(kb, carry):
        there = pl.ds(pl.multiple_of(kb * block, block), block)
        for h in range(heads):
            s = dot_nt(q_ref[:, col[h]], k_ref[there, col[h]])
            old = m_ref[:, col[h]]
            new = jnp.maximum(old, jnp.max(s, axis=1, keepdims=True))
            p = jnp.exp(s - jnp.concatenate([new] * (block // LANES), axis=1)).astype(bf16)
            m_ref[:, col[h]] = new
            acc_ref[:, col[h]] = acc_ref[:, col[h]] * jnp.exp(old - new) + dot_nn(
                p, v_ref[there, col[h]]
            )
        return carry

    lax.fori_loop(begin_ref[at], at, step, 0)
    low = lane < HD
    for t in range((heads + 1) // 2):
        a = acc_ref[:, col[2 * t]]
        b = acc_ref[:, col[2 * t + 1]] if 2 * t + 1 < heads else a
        total = pltpu.roll(jnp.where(low, b, a), HD, 1)
        result = jnp.where(low, a, b) / total
        if 2 * t + 1 >= heads:
            result = jnp.where(low, result, 0.0)
        o_ref[:, t * LANES : (t + 1) * LANES] = result.astype(bf16)
    for h in range(heads):
        a = acc_ref[:, col[h]]
        total = a if h % 2 == 0 else pltpu.roll(a, HD, 1)
        hi, mid, lo = pieces(-(m_ref[:, col[h]] + jnp.log(jnp.where(low, 1.0, total))))
        extra = jnp.where(
            lane == HD + 8, hi, jnp.where(lane == HD + 9, mid, jnp.where(lane == HD + 10, lo, 0.0))
        )
        fill = (lane >= HD + 8) & (lane < HD + 11)
        qo_ref[:, col[h]] = jnp.where(fill, extra, q_ref[:, col[h]].astype(f32)).astype(bf16)


def attend(heads, info, offset, q, k, v, begins, block, rows):
    length = q.shape[0]
    ext = heads * LANES
    width = max(LANES, heads * HD)
    steps = rows // block
    row = lambda i, info, b: (i, 0)
    whole = lambda i, info, b: (0, 0)
    return pl.pallas_call(
        functools.partial(attend_kernel, heads, block, offset, steps),
        name="attend",
        grid_spec=pltpu.PrefetchScalarGridSpec(
            num_scalar_prefetch=2,
            grid=(steps,),
            in_specs=[
                pl.BlockSpec((block, ext), lambda i, info, b: ((info[0] ^ offset) * steps + i, 0)),
                pl.BlockSpec((length, ext), whole),
                pl.BlockSpec((length, ext), whole),
            ],
            out_specs=[pl.BlockSpec((block, width), row), pl.BlockSpec((block, ext), row)],
            scratch_shapes=[pltpu.VMEM((block, ext), f32), pltpu.VMEM((block, ext), f32)],
        ),
        out_shape=[
            jax.ShapeDtypeStruct((rows, width), bf16),
            jax.ShapeDtypeStruct((rows, ext), bf16),
        ],
        compiler_params=pltpu.CompilerParams(vmem_limit_bytes=VMEM),
        cost_estimate=pl.CostEstimate(
            flops=2 * heads * rows * length * LANES,
            bytes_accessed=4 * length * ext,
            transcendentals=heads * rows * length // 2,
        ),
    )(info, begins, q, k, v)


def attend_back_kernel(heads, block, n, info_ref, begin_ref, *refs):
    q_parts, do_parts, o_parts = refs[:n], refs[n : 2 * n], refs[2 * n : 3 * n]
    k_ref, v_ref, cos_ref, sin_ref, g_ref = refs[3 * n : 3 * n + 5]
    sends = refs[3 * n + 5 : 4 * n + 5]
    q_all, do_all, o_all, dk_ref, dv_ref, dq_ref, de_ref, sem = refs[4 * n + 5 :]
    at = pl.program_id(0)
    rows = q_parts[0].shape[0]

    def moves(pairs):
        copies = []
        for i, (make, j) in enumerate(pairs):
            place = pl.ds(pl.multiple_of((info_ref[0] ^ j) * rows, rows), rows)
            copies.append(make(place, sem.at[i]))
        for copy in copies:
            copy.start()
        for copy in copies:
            copy.wait()

    @pl.when(at == 0)
    def _():
        moves(
            [
                (functools.partial(lambda src, dst, p, s: pltpu.make_async_copy(src, dst.at[p], s), part, whole), j)
                for parts, whole in ((q_parts, q_all), (do_parts, do_all), (o_parts, o_all))
                for j, part in enumerate(parts)
            ]
        )

    lane = lax.broadcasted_iota(jnp.int32, (block, LANES), 1)
    r = lax.broadcasted_iota(jnp.int32, (block, block), 0)
    c = lax.broadcasted_iota(jnp.int32, (block, block), 1)
    causal = r <= c
    low = lane < HD
    here = pl.ds(pl.multiple_of(at * block, block), block)
    col = [slice(h * LANES, (h + 1) * LANES) for h in range(heads)]

    for h in range(heads):
        t = slice((h // 2) * LANES, (h // 2 + 1) * LANES)
        own = low if h % 2 == 0 else jnp.logical_not(low)
        grad = do_all[here, t].astype(f32)
        product = grad * o_all[here, t].astype(f32)
        centre = jnp.sum(jnp.where(own, product, 0.0), axis=1, keepdims=True)
        hi, mid, lo = pieces(-jnp.broadcast_to(centre, (block, LANES)))
        spot = lane - (HD if h % 2 == 0 else 0)
        extra = jnp.where(spot == 0, hi, jnp.where(spot == 1, mid, jnp.where(spot == 2, lo, 0.0)))
        de_ref[:, col[h]] = jnp.where(own, grad, extra).astype(bf16)

    def pair(there, h, mask, first):
        st = dot_nt(k_ref[there, col[h]], q_all[here, col[h]])
        p = jnp.exp(st)
        if mask is not None:
            p = jnp.where(mask, p, 0.0)
        dpt = dot_nt(v_ref[there, col[h]], de_ref[:, col[h]])
        ds = (p * dpt).astype(bf16)
        dv = dot_nn(p.astype(bf16), de_ref[:, col[h]])
        dk = dot_nn(ds, q_all[here, col[h]])
        dq = dot_tn(ds, k_ref[there, col[h]])
        if first:
            dv_ref[there, col[h]] = dv
            dk_ref[there, col[h]] = dk
            dq_ref[:, col[h]] = dq
        else:
            dv_ref[there, col[h]] += dv
            dk_ref[there, col[h]] += dk
            dq_ref[:, col[h]] += dq

    for h in range(heads):
        pair(here, h, causal, True)

    def step(kb, carry):
        there = pl.ds(pl.multiple_of(kb * block, block), block)
        for h in range(heads):
            pair(there, h, None, False)
        return carry

    lax.fori_loop(begin_ref[at], at, step, 0)

    def turn_back(ref, rows, scale):
        u1 = u2 = None
        quarter = lane // HALF
        for h in range(heads):
            u = ref[rows, col[h]]
            a = u if h == 0 else pltpu.roll(u, HALF * h, 1)
            b = u if h == 1 else pltpu.roll(u, (LANES + HALF * h - HALF) % LANES, 1)
            u1 = a if h == 0 else jnp.where(quarter == h, a, u1)
            u2 = b if h == 0 else jnp.where(quarter == h, b, u2)
        if heads < GROUP:
            u1 = jnp.where(quarter < heads, u1, 0.0)
            u2 = jnp.where(quarter < heads, u2, 0.0)
        u1, u2 = u1 * scale, u2 * scale
        cs, sn = cos_ref[rows, :], sin_ref[rows, :]
        return (u1 * cs + u2 * sn).astype(bf16), (u2 * cs - u1 * sn).astype(bf16)

    def finish_block(i, carry):
        rows = pl.ds(pl.multiple_of(i * block, block), block)
        d1, d2 = turn_back(dk_ref, rows, 1.0)
        g_ref[rows, 2 * LANES : 3 * LANES] = d1
        g_ref[rows, 3 * LANES : 4 * LANES] = d2
        for t in range((heads + 1) // 2):
            a = dv_ref[rows, col[2 * t]]
            b = dv_ref[rows, col[2 * t + 1]] if 2 * t + 1 < heads else jnp.zeros_like(a)
            d_mix = jnp.where(low, a, b).astype(bf16)
            g_ref[rows, (4 + t) * LANES : (5 + t) * LANES] = (d_mix.astype(f32) * 0.5).astype(bf16)
        return carry

    u1 = u2 = None
    quarter = lane // HALF
    for h in range(heads):
        u = dq_ref[:, col[h]]
        a = u if h == 0 else pltpu.roll(u, HALF * h, 1)
        b = u if h == 1 else pltpu.roll(u, (LANES + HALF * h - HALF) % LANES, 1)
        u1 = a if h == 0 else jnp.where(quarter == h, a, u1)
        u2 = b if h == 0 else jnp.where(quarter == h, b, u2)
    if heads < GROUP:
        u1 = jnp.where(quarter < heads, u1, 0.0)
        u2 = jnp.where(quarter < heads, u2, 0.0)
    u1, u2 = u1 * HD**-0.5, u2 * HD**-0.5
    cs, sn = cos_ref[here, :], sin_ref[here, :]
    g_ref[here, 0:LANES] = (u1 * cs + u2 * sn).astype(bf16)
    g_ref[here, LANES : 2 * LANES] = (u2 * cs - u1 * sn).astype(bf16)

    @pl.when(at == pl.num_programs(0) - 1)
    def _():
        lax.fori_loop(0, pl.num_programs(0), finish_block, 0)
        moves(
            [
                (functools.partial(lambda dst, p, s: pltpu.make_async_copy(g_ref.at[p], dst, s), dst), j)
                for j, dst in enumerate(sends)
            ]
        )


def attend_back(heads, info, q_parts, k, v, do_parts, o_parts, cos, sin, begins, block):
    n = len(q_parts)
    rows = q_parts[0].shape[0]
    length = n * rows
    ext = heads * LANES
    width = o_parts[0].shape[1]
    whole = lambda i, info, b: (0, 0)
    anywhere = pl.BlockSpec(memory_space=pl.ANY)
    columns = 4 * LANES + width
    return pl.pallas_call(
        functools.partial(attend_back_kernel, heads, block, n),
        name="attend_back",
        grid_spec=pltpu.PrefetchScalarGridSpec(
            num_scalar_prefetch=2,
            grid=(length // block,),
            in_specs=[anywhere] * (3 * n)
            + [
                pl.BlockSpec((length, ext), whole),
                pl.BlockSpec((length, ext), whole),
                pl.BlockSpec((length, LANES), whole),
                pl.BlockSpec((length, LANES), whole),
            ],
            out_specs=[pl.BlockSpec((length, columns), whole)] + [anywhere] * n,
            scratch_shapes=[
                pltpu.VMEM((length, ext), bf16),
                pltpu.VMEM((length, width), bf16),
                pltpu.VMEM((length, width), bf16),
                pltpu.VMEM((length, ext), f32),
                pltpu.VMEM((length, ext), f32),
                pltpu.VMEM((block, ext), f32),
                pltpu.VMEM((block, ext), bf16),
                pltpu.SemaphoreType.DMA((3 * n,)),
            ],
        ),
        out_shape=[jax.ShapeDtypeStruct((length, columns), bf16)]
        + [jax.ShapeDtypeStruct((rows, columns), bf16)] * n,
        compiler_params=pltpu.CompilerParams(vmem_limit_bytes=VMEM),
        cost_estimate=pl.CostEstimate(
            flops=5 * heads * length * length * LANES,
            bytes_accessed=2 * 8 * length * ext,
            transcendentals=heads * length * length // 2,
        ),
    )(info, begins, *q_parts, *do_parts, *o_parts, k, v, cos, sin)


def split_axis(n):
    low = 1 << ((n.bit_length() - 1) // 2)
    return n // low, low


def swap(axis, value, offset):
    n = lax.axis_size(axis)
    return lax.ppermute(value, axis, [(i, i ^ offset) for i in range(n)])


def gather_rows(value, n):
    high, low = split_axis(n)
    rows = value.shape[0]
    half = rows // 2
    parts = {0: value}
    for b in range(1, low):
        parts[b] = swap("tensor", value, b)
    for a in range(1, high):
        parts[a * low] = swap("tensor", value, a * low)
    listed = [(parts[j], j, 0) for j in sorted(parts)]
    for a in range(1, high):
        for b in range(1, low):
            j = a * low + b
            listed.append((swap("tensor", parts[b][:half], a * low), j, 0))
            listed.append((swap("tensor", parts[a * low][half:], b), j, half))
    return listed


def after(value, *others):
    return lax.optimization_barrier((value,) + others)[0]


def add_up(first, *others):
    total = first.astype(f32)
    for other in others:
        total = total + other.astype(f32)
    return total


def halve_over_z(parts, z, count):
    step = 1
    while step < count:
        pairs = parts.reshape((-1, 2) + parts.shape[1:])
        side = (z // step) % 2
        pick = lambda which: lax.dynamic_index_in_dim(pairs, which, 1, keepdims=False)
        parts = add_up(pick(side), swap("dp", pick(1 - side), 2 * step))
        parts = parts.astype(bf16) if 2 * step < count else parts
        given = yield parts
        parts = parts if given is None else given
        step *= 2


def all_sum(value, axis):
    n = lax.axis_size(axis)
    step = 1
    while step < n:
        value = value + swap(axis, value, step)
        step *= 2
    return value


def anywhere():
    return pl.BlockSpec(memory_space=pl.ANY)


def norm_kernel(x_ref, gain_ref, o_ref):
    x = x_ref[...].astype(f32)
    inverse = lax.rsqrt(jnp.mean(x * x, axis=-1, keepdims=True) + EPS)
    o_ref[...] = (x * inverse * gain_ref[...]).astype(bf16)


def norm_rows(x, gain):
    rows, depth = x.shape
    block = min(rows, 128)
    return pl.pallas_call(
        norm_kernel,
        name="norm_rows",
        grid=(rows // block,),
        in_specs=[
            pl.BlockSpec((block, depth), lambda i: (i, 0)),
            pl.BlockSpec((1, depth), lambda i: (0, 0)),
        ],
        out_specs=pl.BlockSpec((block, depth), lambda i: (i, 0)),
        out_shape=jax.ShapeDtypeStruct((rows, depth), bf16),
        compiler_params=pltpu.CompilerParams(vmem_limit_bytes=VMEM),
        cost_estimate=pl.CostEstimate(
            flops=5 * x.size, bytes_accessed=4 * x.size, transcendentals=rows
        ),
    )(x, gain)


def branch_kernel(n, first, info_ref, *refs):
    att = refs[:n]
    w_ref, tok_ref, gain_ref, mid_ref, h_ref, all_ref, sem = refs[n:]
    size = tok_ref.shape[0]
    width = att[0].shape[1]
    copies = []
    for j in range(n):
        lanes = pl.ds(pl.multiple_of((info_ref[0] ^ j) * width, width), width)
        copies.append(
            pltpu.make_async_copy(att[j].at[first : first + size, :], all_ref.at[:, lanes], sem.at[j])
        )
    for copy in copies:
        copy.start()
    for copy in copies:
        copy.wait()
    x = tok_ref[...].astype(f32) + dot_nn(all_ref[...], w_ref[...])
    mid_ref[...] = x
    inverse = lax.rsqrt(jnp.mean(x * x, axis=-1, keepdims=True) + EPS)
    h_ref[...] = (x * inverse * gain_ref[...]).astype(bf16)


def branch(info, att, w_all, tokens, gain, first, size):
    n = len(att)
    width = att[0].shape[1]
    depth = tokens.shape[1]
    at = first // size
    whole = lambda i, info: (0, 0)
    return pl.pallas_call(
        functools.partial(branch_kernel, n, first),
        name="branch",
        grid_spec=pltpu.PrefetchScalarGridSpec(
            num_scalar_prefetch=1,
            grid=(1,),
            in_specs=[anywhere()] * n
            + [
                pl.BlockSpec(w_all.shape, whole),
                pl.BlockSpec((size, depth), lambda i, info: (at, 0)),
                pl.BlockSpec((1, depth), whole),
            ],
            out_specs=[pl.BlockSpec((size, depth), whole)] * 2,
            scratch_shapes=[pltpu.VMEM((size, n * width), bf16), pltpu.SemaphoreType.DMA((n,))],
        ),
        out_shape=[
            jax.ShapeDtypeStruct((size, depth), f32),
            jax.ShapeDtypeStruct((size, depth), bf16),
        ],
        compiler_params=pltpu.CompilerParams(vmem_limit_bytes=VMEM),
        cost_estimate=pl.CostEstimate(
            flops=2 * size * depth * n * width,
            bytes_accessed=2 * n * width * depth + 8 * size * depth,
            transcendentals=size,
        ),
    )(info, *att, w_all, tokens, gain)


def feed_kernel(shards_in, joined, send, info_ref, h_ref, g_ref, *refs):
    flat = [ref for shard in shards_in for ref in range(shard)]
    weights, refs = refs[: len(flat)], refs[len(flat) :]
    if joined:
        (out_in, dh_in), refs = refs[:2], refs[2:]
    out_ref, dh_ref, act_ref, w_ref, sem = refs[:5]
    out_acc, dh_acc = refs[5:] if send else (out_ref, dh_ref)
    high, rows_w, depth = w_ref.shape
    units = rows_w // 3
    copies, at = [], 0
    for a, count in enumerate(shards_in):
        group = []
        for i in range(count):
            ref = weights[at]
            if count == 3:
                group.append(
                    pltpu.make_async_copy(ref, w_ref.at[a, pl.ds(i * units, units)], sem.at[at])
                )
            elif len(ref.shape) == 3:
                size = ref.shape[2]
                for d in range(ref.shape[0]):
                    group.append(
                        pltpu.make_async_copy(
                            ref.at[d],
                            w_ref.at[a, :, d * size : (d + 1) * size],
                            sem.at[len(flat) + a * ref.shape[0] + d],
                        )
                    )
            else:
                group.append(pltpu.make_async_copy(ref, w_ref.at[a], sem.at[at]))
            at += 1
        copies.append(group)
    first = pl.program_id(0) == 0

    @pl.when(first)
    def _():
        for group in copies:
            for copy in group:
                copy.start()

    for a in range(high):

        @pl.when(first)
        def _():
            for copy in copies[a]:
                copy.wait()

        gate_w, up_w, down_w = (w_ref.at[a, pl.ds(m * units, units)] for m in range(3))
        gate = dot_nt(h_ref[...], gate_w[...])
        up = dot_nt(h_ref[...], up_w[...])
        back = dot_nt(g_ref[...], down_w[...])
        s = 1.0 / (1.0 + jnp.exp(-gate))
        gs = gate * s
        hidden = (gs * up).astype(bf16)
        d_up = (back * gs).astype(bf16)
        d_gate = (back * up * (s + gs * (1.0 - s))).astype(bf16)
        act_ref[a, 0] = d_gate
        act_ref[a, 1] = d_up
        act_ref[a, 2] = hidden
        part = dot_nn(hidden, down_w[...])
        d_part = dot_nn(d_gate, gate_w[...]) + dot_nn(d_up, up_w[...])
        if a == 0 and joined:
            out_acc[...] = out_in[...] + part
            dh_acc[...] = dh_in[...] + d_part
        elif a == 0:
            out_acc[...] = part
            dh_acc[...] = d_part
        else:
            out_acc[...] += part
            dh_acc[...] += d_part
    if send:
        out_ref[...] = out_acc[...].astype(bf16)
        dh_ref[...] = dh_acc[...].astype(bf16)


def feed(info, h, g, g_first, weights, sums, send):
    rows, depth = h.shape
    high = len(weights)
    flat = [w for shard in weights for w in shard]
    units = weights[0][0].shape[0] if len(weights[0]) == 3 else weights[0][0].shape[-2] // 3
    block = min(rows, 256)
    at = g_first // block
    row = lambda i, info: (i, 0)
    kind = bf16 if send else f32
    slices = max(w.shape[0] if w.ndim == 3 else 0 for w in flat)
    return pl.pallas_call(
        functools.partial(feed_kernel, tuple(len(shard) for shard in weights), bool(sums), send),
        name="feed",
        grid_spec=pltpu.PrefetchScalarGridSpec(
            num_scalar_prefetch=1,
            grid=(rows // block,),
            in_specs=[
                pl.BlockSpec((block, depth), row),
                pl.BlockSpec((block, depth), lambda i, info: (at + i, 0)),
            ]
            + [anywhere()] * len(flat)
            + [pl.BlockSpec((block, depth), row)] * len(sums),
            out_specs=[pl.BlockSpec((block, depth), row)] * 2
            + [pl.BlockSpec((high, 3, block, units), lambda i, info: (0, 0, i, 0))],
            scratch_shapes=[
                pltpu.VMEM((high, 3 * units, depth), bf16),
                pltpu.SemaphoreType.DMA((len(flat) + high * slices,)),
            ]
            + ([pltpu.VMEM((block, depth), f32)] * 2 if send else []),
        ),
        out_shape=[
            jax.ShapeDtypeStruct((rows, depth), kind),
            jax.ShapeDtypeStruct((rows, depth), kind),
            jax.ShapeDtypeStruct((high, 3, rows, units), bf16),
        ],
        compiler_params=pltpu.CompilerParams(vmem_limit_bytes=VMEM),
        cost_estimate=pl.CostEstimate(
            flops=12 * rows * depth * high * units,
            bytes_accessed=6 * depth * high * units + 12 * rows * depth,
            transcendentals=2 * rows * high * units,
        ),
    )(info, h, g, *flat, *sums)


def feed_grad_kernel(parts, members, info_ref, *refs):
    h, g, acts = refs[:parts], refs[parts : 2 * parts], refs[2 * parts : 3 * parts]
    keep_ref, send_ref, acc_ref = refs[3 * parts :]
    core = info_ref[1]

    def product(sources):
        return sum(dot_tn(acts[p][0, 0], sources[p][...]) for p in range(parts))

    @pl.when(pl.program_id(1) < 2)
    def _():
        acc_ref[...] = product(h)

    @pl.when(pl.program_id(1) == 2)
    def _():
        acc_ref[...] = product(g)

    size = acc_ref.shape[1] // (2 * members)
    for z in range(members):
        for ref, side in ((keep_ref, core), (send_ref, 1 - core)):
            pair = acc_ref[:, 2 * z * size : 2 * (z + 1) * size]
            ref[0, z, 0] = jnp.where(side == 0, pair[:, :size], pair[:, size:]).astype(bf16)


def feed_grads(info, h, g, g_at, acts, firsts, high, members):
    parts = len(h)
    depth = h[0].shape[1]
    units = acts[0].shape[3]
    size = depth // (2 * members)
    whole = lambda a, m, info: (0, 0)
    out = jax.ShapeDtypeStruct((high, members, 3, units, size), bf16)
    return pl.pallas_call(
        functools.partial(feed_grad_kernel, parts, members),
        name="feed_grads",
        grid_spec=pltpu.PrefetchScalarGridSpec(
            num_scalar_prefetch=1,
            grid=(high, 3),
            in_specs=[pl.BlockSpec(v.shape, whole) for v in h]
            + [
                pl.BlockSpec(v.shape, lambda a, m, info, at=at: (at, 0)) for v, at in zip(h, g_at)
            ]
            + [
                pl.BlockSpec((1, 1, v.shape[2], units), lambda a, m, info, f=f: (a + f, m, 0, 0))
                for v, f in zip(acts, firsts)
            ],
            out_specs=[
                pl.BlockSpec((1, members, 1, units, size), lambda a, m, info: (a, 0, m, 0, 0))
            ]
            * 2,
            scratch_shapes=[pltpu.VMEM((units, depth), f32)],
        ),
        out_shape=[out, out],
        compiler_params=pltpu.CompilerParams(vmem_limit_bytes=VMEM),
        cost_estimate=pl.CostEstimate(
            flops=6 * high * sum(v.shape[0] for v in h) * depth * units,
            bytes_accessed=12 * high * depth * units,
            transcendentals=0,
        ),
    )(info, *h, *g, *acts)


def branch_back_kernel(n, parts, info_ref, *refs):
    dh, far = refs[:parts], refs[parts : 2 * parts]
    mid = refs[2 * parts : 3 * parts]
    first_ref, g_ref, gain_ref, w_ref = refs[3 * parts : 3 * parts + 4]
    dm_ref, db_ref, gg_ref = refs[3 * parts + 4 : 3 * parts + 7]
    da = refs[3 * parts + 7 :]
    rows = mid[0].shape[0]
    width = da[0].shape[1]
    for p in range(parts):
        at = slice(p * rows, (p + 1) * rows)
        x = mid[p][...]
        inverse = lax.rsqrt(jnp.mean(x * x, axis=-1, keepdims=True) + EPS)
        unit = x * inverse
        cotangent = dh[p][...] + far[p][...].astype(f32)
        e = cotangent * gain_ref[...]
        inner = jnp.mean(e * unit, axis=-1, keepdims=True)
        d_mid = g_ref[at, :].astype(f32) + inverse * (e - unit * inner)
        share = jnp.sum(cotangent * unit, axis=0, keepdims=True)
        gg_ref[...] = share if p == 0 else gg_ref[...] + share
        dm_ref[at, :] = d_mid
        db_ref[at, :] = d_mid.astype(bf16)
    for j in range(n):
        place = pl.ds(pl.multiple_of((info_ref[0] ^ j) * width, width), width)
        da[j][...] = dot_nt(db_ref[...], w_ref[place, :]).astype(bf16)


def branch_back(info, d_h, d_far, middle, g, gain, w_all, width):
    n = w_all.shape[0] // width
    parts = len(middle)
    rows, depth = middle[0].shape
    whole = lambda i, info: (0, 0)
    part = lambda p: pl.BlockSpec((rows, depth), lambda i, info, p=p: (p, 0))
    shapes = [((parts * rows, depth), f32), ((parts * rows, depth), bf16), ((1, depth), f32)]
    shapes += [((parts * rows, width), bf16)] * n
    return pl.pallas_call(
        functools.partial(branch_back_kernel, n, parts),
        name="branch_back",
        grid_spec=pltpu.PrefetchScalarGridSpec(
            num_scalar_prefetch=1,
            grid=(1,),
            in_specs=[part(p) for p in range(parts)]
            + [pl.BlockSpec((rows, depth), whole)] * (2 * parts)
            + [
                pl.BlockSpec((1, LANES), whole),
                pl.BlockSpec(g.shape, whole),
                pl.BlockSpec(gain.shape, whole),
                pl.BlockSpec(w_all.shape, whole),
            ],
            out_specs=[pl.BlockSpec(s, whole) for s, _ in shapes],
        ),
        out_shape=[jax.ShapeDtypeStruct(s, d) for s, d in shapes],
        compiler_params=pltpu.CompilerParams(vmem_limit_bytes=VMEM),
        cost_estimate=pl.CostEstimate(
            flops=2 * parts * rows * depth * n * width,
            bytes_accessed=20 * parts * rows * depth + 2 * n * width * depth,
            transcendentals=parts * rows,
        ),
    )(info, *[d_h] * parts, *d_far, *middle, jnp.zeros((1, LANES), f32), g, gain, w_all)


def out_grad_kernel(n, info_ref, *refs):
    db_ref = refs[0]
    att = refs[1 : 1 + n]
    o_ref = refs[1 + n]
    width = att[0].shape[1]
    for j in range(n):
        place = pl.ds(pl.multiple_of((info_ref[0] ^ j) * width, width), width)
        o_ref[place, :] = dot_tn(att[j][...], db_ref[...]).astype(bf16)


def out_grads(info, d_branch, att):
    n = len(att)
    rows, depth = d_branch.shape
    width = att[0].shape[1]
    whole = lambda i, info: (0, 0)
    return pl.pallas_call(
        functools.partial(out_grad_kernel, n),
        name="out_grads",
        grid_spec=pltpu.PrefetchScalarGridSpec(
            num_scalar_prefetch=1,
            grid=(1,),
            in_specs=[pl.BlockSpec(d_branch.shape, whole)]
            + [pl.BlockSpec(a.shape, whole) for a in att],
            out_specs=pl.BlockSpec((n * width, depth), whole),
        ),
        out_shape=jax.ShapeDtypeStruct((n * width, depth), bf16),
        compiler_params=pltpu.CompilerParams(vmem_limit_bytes=VMEM),
        cost_estimate=pl.CostEstimate(
            flops=2 * rows * depth * n * width,
            bytes_accessed=2 * rows * depth + 4 * n * width * depth,
            transcendentals=0,
        ),
    )(info, d_branch, *att)


def qkv_grad_kernel(x_ref, d_ref, w_ref, sel_ref, o_ref, share_ref):
    g = dot_tn(x_ref[...], d_ref[...])
    share_ref[...] = jnp.sum(g * w_ref[...].astype(f32), axis=1, keepdims=True)
    o_ref[...] = dot_nt(g.astype(bf16), sel_ref[...]).astype(bf16)


def qkv_grads(x, d, w, select):
    length, depth = x.shape
    columns = select.shape[0]
    block = 512
    whole = lambda i: (0, 0)
    return pl.pallas_call(
        qkv_grad_kernel,
        name="qkv_grads",
        grid=(depth // block,),
        in_specs=[
            pl.BlockSpec((length, block), lambda i: (0, i)),
            pl.BlockSpec(d.shape, whole),
            pl.BlockSpec((block, w.shape[1]), lambda i: (i, 0)),
            pl.BlockSpec(select.shape, whole),
        ],
        out_specs=[
            pl.BlockSpec((block, columns), lambda i: (i, 0)),
            pl.BlockSpec((block, 1), lambda i: (i, 0)),
        ],
        out_shape=[
            jax.ShapeDtypeStruct((depth, columns), bf16),
            jax.ShapeDtypeStruct((depth, 1), f32),
        ],
        compiler_params=pltpu.CompilerParams(vmem_limit_bytes=VMEM),
        cost_estimate=pl.CostEstimate(
            flops=2 * length * depth * d.shape[1],
            bytes_accessed=2 * (x.size + d.size + 2 * w.size),
            transcendentals=0,
        ),
    )(x, d, w, select)


def finish_kernel(n, wide, info_ref, *refs):
    d = refs[:n]
    cols_ref, tok_ref, gain_ref, dm_ref, o_ref = refs[n : n + 5]
    w_ref, sem = refs[-2:]
    t = info_ref[0]
    members, _, size, columns = cols_ref.shape
    depth = members * size
    first = pl.program_id(0) == 0
    copies = [
        pltpu.make_async_copy(cols_ref.at[:, j], w_ref.at[j], sem.at[j]) for j in range(n)
    ]

    @pl.when(first)
    def _():
        for copy in copies:
            copy.start()

    for j in range(n):

        @pl.when(first)
        def _():
            copies[j].wait()

        part = dot_nt(d[j][...], w_ref[j].reshape(depth, columns))
        o_ref[...] = part if j == 0 else o_ref[...] + part
    x = tok_ref[...].astype(f32)
    inverse = lax.rsqrt(jnp.mean(x * x, axis=-1, keepdims=True) + EPS)
    unit = x * inverse
    e = o_ref[...] * gain_ref[...]
    inner = jnp.mean(e * unit, axis=-1, keepdims=True)
    o_ref[...] = dm_ref[...] + inverse * (e - unit * inner)
    if wide:
        first_ref = refs[n + 5]
        width = depth // n
        for j in range(n):
            at = pl.ds(pl.multiple_of((t ^ j) * width, width), width)
            first_ref[:, at] = d[j][:, 4 * LANES :].astype(f32)


def finish(info, d_parts, cols, tokens, gain, d_middle):
    n = len(d_parts)
    rows, depth = tokens.shape
    block = min(rows, 256)
    wide = (depth // n) % LANES == 0
    row = lambda i, info: (i, 0)
    whole = lambda i, info: (0, 0)
    count = 2 if wide else 1
    members, _, size, columns = cols.shape
    out = pl.pallas_call(
        functools.partial(finish_kernel, n, wide),
        name="finish",
        grid_spec=pltpu.PrefetchScalarGridSpec(
            num_scalar_prefetch=1,
            grid=(rows // block,),
            in_specs=[pl.BlockSpec((block, d.shape[1]), row) for d in d_parts]
            + [
                anywhere(),
                pl.BlockSpec((block, depth), row),
                pl.BlockSpec((1, depth), whole),
                pl.BlockSpec((block, depth), row),
            ],
            out_specs=[pl.BlockSpec((block, depth), row)] * count,
            scratch_shapes=[
                pltpu.VMEM((n, members, size, columns), bf16),
                pltpu.SemaphoreType.DMA((n,)),
            ],
        ),
        out_shape=[jax.ShapeDtypeStruct((rows, depth), f32)] * count,
        compiler_params=pltpu.CompilerParams(vmem_limit_bytes=VMEM),
        cost_estimate=pl.CostEstimate(
            flops=2 * rows * cols.size,
            bytes_accessed=2 * cols.size + 16 * rows * depth,
            transcendentals=rows,
        ),
    )(info, *d_parts, cols, tokens, gain, d_middle)
    if wide:
        return out
    heads_width = depth // n
    pieces_ = jnp.stack([d[:, 4 * LANES : 4 * LANES + heads_width] for d in d_parts])
    ordered = jnp.take(pieces_, info[0] ^ jnp.arange(n), axis=0)
    return out[0], ordered.transpose(1, 0, 2).reshape(rows, depth).astype(f32)


def shards(
    tokens,
    first_values,
    doc_lengths,
    attention_norm_gain,
    w_qkv,
    w_out,
    feedforward_norm_gain,
    w_gate,
    w_up,
    w_down,
    out_grad,
):
    n = lax.axis_size("tensor")
    high, low = split_axis(n)
    members = lax.axis_size("dp") // 2
    t = lax.axis_index("tensor")
    z, core = lax.axis_index("dp") // 2, lax.axis_index("dp") % 2
    info = jnp.stack([t, core]).astype(jnp.int32)
    rows, depth = tokens.shape
    heads = w_out.shape[0] // HD
    own_width = heads * HD
    width = max(LANES, own_width)
    length = rows * n
    block = min(256, rows)
    gain_one = attention_norm_gain[None, :]
    gain_two = feedforward_norm_gain[None, :]
    missing = width - own_width
    widen = lambda v: jnp.pad(v, ((0, 0), (0, missing))) if missing else v
    replicas = 2 * members
    size_d = depth // replicas
    mine = lambda w, axis: lax.dynamic_slice_in_dim(w, lax.axis_index("dp") * size_d, size_d, axis)

    together = lax.optimization_barrier
    cosine, sine_table = rope_tables(length)
    ends = jnp.cumsum(doc_lengths[0])
    starts = ends - doc_lengths[0]
    docs = doc_lengths.shape[1]
    limits = jnp.pad(jnp.stack([starts, ends]), ((0, 6), (HD, LANES - HD - docs)))
    heads_at = jnp.arange(length // block, dtype=jnp.int32) * block
    begins = jnp.max(jnp.where(starts[None, :] <= heads_at[:, None], starts[None, :], 0), axis=1)
    begins = (begins // block).astype(jnp.int32)
    select = column_selector(heads)
    w_cols = jnp.dot(w_qkv, select, preferred_element_type=f32).astype(bf16)

    own_weights = (w_gate.T, w_up.T, w_down)
    weight_slice = jnp.concatenate([mine(w, 1) for w in own_weights])
    normed = norm_rows(tokens, gain_one)
    normed_parts = gather_rows(normed, n)
    value_part = lambda j: widen(
        lax.dynamic_slice_in_dim(first_values, (t ^ j) * own_width, own_width, 1)
    )
    value_parts = [value_part(0)] + [swap("tensor", value_part(j), j) for j in range(1, n)]
    w_out_wide = jnp.pad(w_out, ((0, missing), (0, 0))) if missing else w_out
    placed = [(j, first) for _, j, first in normed_parts]
    pieces_in = [piece for piece, _, _ in normed_parts]
    cols_slice = mine(w_cols, 0)
    (
        pieces_in, value_parts, weight_slice, w_cols, cols_slice, cosine, sine_table, limits,
        w_out_late, grad_late,
    ) = together(
        (
            pieces_in, value_parts, weight_slice, w_cols, cols_slice, cosine, sine_table, limits,
            w_out_wide, out_grad,
        )
    )

    w_out_all = lax.all_gather(w_out_late, "tensor", axis=0, tiled=True)
    far_slices = [swap("tensor", weight_slice, a * low) for a in range(1, high)]
    cols_far = [cols_slice] + [swap("tensor", cols_slice, j) for j in range(1, n)]
    grad_rows = [out_grad] + [swap("tensor", grad_late, b) for b in range(1, low)]
    normed_parts = [(piece, j, first) for piece, (j, first) in zip(pieces_in, placed)]
    q, k, v, squares, normed_all = project(
        heads, info, normed_parts, value_parts, w_cols, cosine, sine_table, limits, rows
    )
    q, far_slices, cols_far = together((q, far_slices, cols_far))
    if size_d % LANES == 0:
        feed_far = [(lax.all_gather(w, "dp", axis=0),) for w in far_slices]
    else:
        feed_far = [(lax.all_gather(w, "dp", axis=1, tiled=True),) for w in far_slices]
    seen = {}
    for j in range(n - 1, -1, -1):
        if j == 0:
            w_out_all, q, *grad_rows = together((w_out_all, q, *grad_rows))
        seen[j] = attend(heads, info, j, q, k, v, begins, block, rows)
    heads_rows = [seen[0][0]] + [swap("tensor", seen[j][0], j) for j in range(1, n)]
    heads_rows, cols = together((heads_rows, jnp.stack(cols_far)))

    cols = lax.all_gather(cols, "dp", axis=0)
    parts = 2 if rows >= 512 else 1
    size = rows // parts
    middle, second = zip(
        *[
            branch(info, heads_rows, w_out_all, tokens, gain_two, p * size, size)
            for p in range(parts)
        ]
    )
    far_keys = [(b, p) for b in range(1, low) for p in range(parts)]
    inputs = {key: swap("tensor", second[key[1]], key[0]) for key in far_keys}
    second_all = jnp.concatenate(second) if parts > 1 else second[0]
    *own_sums, own_acts = feed(info, second_all, out_grad, 0, [own_weights], [], False)
    own_out, own_back, far_acts = feed(info, second_all, out_grad, 0, feed_far, own_sums, False)
    fed = {}
    last = own_out
    for b, p in far_keys:
        arrived, last = together((inputs[b, p], last))
        fed[b, p] = feed(
            info, arrived, grad_rows[b], p * size, [own_weights] + feed_far, [], True
        )
        inputs[b, p] = arrived
    own_out = last
    d_far = [[swap("tensor", fed[b, p][1], b) for b in range(1, low)] for p in range(parts)]
    d_far = [d[0] if low == 2 else add_up(*d) for d in d_far]
    sources = (
        [second_all] + [inputs[key] for key in far_keys],
        [out_grad] + [grad_rows[b] for b, p in far_keys],
        [0] + [p for b, p in far_keys],
    )
    far_parts = [fed[key][2] for key in far_keys]
    count = len(far_keys)
    far_keep, far_send = feed_grads(
        info, *sources, [far_acts] + far_parts, [0] + [1] * count, high - 1, members
    )
    own_keep, own_send = feed_grads(
        info, *sources, [own_acts] + far_parts, [0] * (count + 1), 1, members
    )
    d_far, far_send, own_send, far_keep, own_keep = together(
        (d_far, far_send, own_send, far_keep, own_keep)
    )

    far_got, own_got = swap("dp", far_send, 1), swap("dp", own_send, 1)
    d_middle, d_branch, feed_share, *d_att = branch_back(
        info, own_back, d_far, middle, out_grad, gain_two, w_out_all, width
    )
    d_att = [d_att[0]] + [swap("tensor", d_att[j], j) for j in range(1, n)]
    pair = lambda a, lo, hi: (
        (own_keep[0, :, lo:hi], own_got[0, :, lo:hi])
        if a == 0
        else (far_keep[a - 1, :, lo:hi], far_got[a - 1, :, lo:hi])
    )
    gate_sums = jnp.concatenate(
        [add_up(*pair(a, 0, 1)).astype(bf16) for a in range(high)], axis=1
    )
    rest_sums = [add_up(*pair(a, 1, 3)).astype(bf16) for a in range(high)]
    out_grad_w = out_grads(info, d_branch, heads_rows)
    out_parts = [
        jnp.concatenate([fed[b, p][0] for p in range(parts)]) if parts > 1 else fed[b, 0][0]
        for b in range(1, low)
    ]
    d_att, gate_sums, rest_sums, out_parts, out_grad_w = together(
        (d_att, gate_sums, rest_sums, out_parts, out_grad_w)
    )

    gate_z = [
        swap("dp", lax.dynamic_index_in_dim(gate_sums, z ^ k, 0, keepdims=False), 2 * k)
        for k in range(1, members)
    ]
    rest_got = [swap("tensor", rest_sums[a], a * low) for a in range(1, high)]
    out_got = [swap("tensor", v_, b) for b, v_ in zip(range(1, low), out_parts)]
    out_sum = lax.psum_scatter(out_grad_w, "dp", scatter_dimension=1, tiled=True)
    d_cols = attend_back(
        heads, info, [seen[j][1] for j in range(n)], k, v, d_att, [seen[j][0] for j in range(n)],
        cosine, sine_table, begins, block,
    )
    d_cols, gate_z, rest_got, out_got, cols, rest_own = together(
        (d_cols, gate_z, rest_got, out_got, cols, rest_sums[0])
    )

    d_all, *d_parts = d_cols
    rest_sum = add_up(rest_own, *rest_got).astype(bf16)
    d_parts, d_all, rest_sum = together((d_parts, d_all, rest_sum))
    d_parts = [d_parts[0]] + [swap("tensor", d_parts[j], j) for j in range(1, n)]
    rest_steps = halve_over_z(rest_sum, z, members)
    rest_sum = next(rest_steps)
    qkv_grad, share = qkv_grads(normed_all, d_all, w_cols, select)
    qkv_sum = lax.psum_scatter(qkv_grad, "dp", scatter_dimension=0, tiled=True)
    gate_sum = add_up(
        lax.dynamic_index_in_dim(gate_sums, z, 0, keepdims=False), *gate_z
    ).astype(bf16)
    gate_sum = add_up(
        gate_sum[0], *[swap("tensor", gate_sum[a], a * low) for a in range(1, high)]
    )
    middle_all = jnp.concatenate(middle) if parts > 1 else middle[0]
    out = add_up(middle_all, own_out, *out_got).astype(bf16)
    totals = jnp.sum(squares[:2], axis=1)
    scalars = jnp.pad(totals[None, :], ((0, 0), (0, depth - 2)))
    shares = jnp.concatenate([share.reshape(1, depth) / gain_one, feed_share, scalars])
    d_parts, shares, rest_sum, gate_sum, out = together((d_parts, shares, rest_sum, gate_sum, out))
    rest_sum = rest_steps.send(rest_sum)
    for rest_sum in rest_steps:
        pass
    sums = all_sum(all_sum(shares, "tensor"), "dp")
    out_sum = lax.psum_scatter(out_sum, "tensor", scatter_dimension=0, tiled=True)
    tokens_grad, first_grad = finish(info, d_parts, cols, tokens, gain_one, d_middle)
    entry_count = first_values.size * lax.axis_size("dp") * n
    return (
        out,
        tokens_grad,
        first_grad,
        sums[0],
        qkv_sum.astype(f32),
        out_sum[:own_width].astype(f32),
        sums[1],
        gate_sum.T,
        rest_sum[0, 0].T,
        rest_sum[0, 1],
        jnp.sqrt(sums[2, 1] / entry_count),
        jnp.sqrt(sums[2, 0] / entry_count),
    )


def solution(mesh):
    token_spec = P(("dp", "tensor"), None)
    return jax.shard_map(
        shards,
        mesh=mesh,
        in_specs=(
            token_spec,
            token_spec,
            P("dp", None),
            P(),
            P(None, "tensor"),
            P("tensor", None),
            P(),
            P(None, "tensor"),
            P(None, "tensor"),
            P("tensor", None),
            token_spec,
        ),
        out_specs=(
            token_spec,
            token_spec,
            token_spec,
            P(),
            P("dp", "tensor"),
            P("tensor", "dp"),
            P(),
            P("dp", "tensor"),
            P("dp", "tensor"),
            P("tensor", "dp"),
            P(),
            P(),
        ),
        check_vma=False,
    )
```

time: 712 us -> 432 us (0.61)
  waiting for transfers between devices: 417 us -> 80.2 us
  Pallas kernels: 69 us -> 211 us
  matrix products: 91 us -> 1.44 us
  starting transfers between devices: 9.81 us -> 55.4 us
  blocking collectives: 39.8 us -> 0 us
    reduce_scatter x5 -> x2, waiting for transfers between devices: 204 us -> 0.01 us  [the longest x1 0.01 us: shards(): lax.psum_scatter(out_sum, 'tensor', scatter_dimension=0, tiled=True)]
    all_gather x4 -> x3, waiting for transfers between devices: 156 us -> 2.6 us  [the longest x1 2.57 us: shards(): feed_far = [(lax.all_gather(w, 'dp', axis=0),) for w in far_slices]]
    pallas_call x3 -> x19, Pallas kernels: 69 us -> 211 us  [the longest x4 46 us: feed(): pl.pallas_call(functools.partial(feed_kernel, tuple((len(shard) for shard...]
    dot_general x14 -> x0, matrix products: 88.3 us -> none  [the longest x1 11.8 us: shards(): jnp.einsum('td,fd->tf', out_rows, down_full, preferred_element_type=f32)]
    ppermute x0 -> x40, waiting for transfers between devices: none -> 76 us  [swap(): return lax.ppermute(value, axis, [(i, i ^ offset) for i in range(n)])]
    ppermute x0 -> x40, starting transfers between devices: none -> 54.5 us  [swap(): return lax.ppermute(value, axis, [(i, i ^ offset) for i in range(n)])]
    unnamed x17 -> x7, waiting for transfers between devices: 48.9 us -> 1.55 us
    psum x1 -> x0, blocking collectives: 39.8 us -> none  [shards(): lax.psum((attention_gain_share, feedforward_gain_share, jnp.sum(squares[0...]
  transfers between devices with their start and end apart: 15 -> 46, of which waited for: 12 -> 14; matrix products, arithmetic and copies ran while one was open for 14% -> 12% of each run, Pallas kernels for 6% -> 49%
where the time goes in v2:
time: 432 us; the launch traced here: 424 us
  Pallas kernels  211 us (49%)
  waiting for transfers between devices  80.2 us (19%)
  starting transfers between devices  55.4 us (13%)
  other arithmetic  35.2 us (8%)
  local copies, waits for them, and re-layouts  22 us (5%)
  between operations  18.9 us (4%)
    ppermute x40, waiting for transfers between devices, swap(): return lax.ppermute(value, axis, [(i, i ^ offset) for i in range(n)])  76 us
    ppermute x40, starting transfers between devices, swap(): return lax.ppermute(value, axis, [(i, i ^ offset) for i in range(n)])  54.5 us
    pallas_call x4, Pallas kernels, feed(): pl.pallas_call(functools.partial(feed_kernel, tuple((len(shard) for shard...  46 us
    pallas_call x1, Pallas kernels, attend_back(): pl.pallas_call(functools.partial(attend_back_kernel, heads, block, n), na...  45.8 us
    pallas_call x4, Pallas kernels, attend(): pl.pallas_call(functools.partial(attend_kernel, heads, block, offset, ste...  37 us
    pallas_call x2, Pallas kernels, feed_grads(): pl.pallas_call(functools.partial(feed_grad_kernel, parts, members), name=...  21.6 us
    pallas_call x1, Pallas kernels, project(): pl.pallas_call(functools.partial(project_kernel, heads, n, rows, placed),...  12.1 us
    pallas_call x2, Pallas kernels, branch(): pl.pallas_call(functools.partial(branch_kernel, n, first), name='branch',...  10.9 us
  transfers between devices with their start and end apart: 46, of which 14 were waited for; matrix products, arithmetic and copies ran while one was open for 12% of the time, Pallas kernels for 49%

profile of v2, /device:TPU:0, one launch (start us, length us, event | category | flops | bytes accessed | tf_op | source)
XLA Modules:
  0.0 423.9 jit_solution(1050208890691121187)
XLA Ops:
  7.3 3.8 norm_rows.1.refs_0_
  11.1 2.9 collective-permute-start
  16.9 3.0 collective-permute-start.6
  24.7 3.9 fusion.9
  28.6 9.7 %collective-permute-done.refs_1_ = bf16[512,1024]{1,0:T(8,128)(2,1)} collective-permute-done((bf16[512,1024]{1,0:T(8,128)(2,1)}, bf16[512,1024]{1,0:T(8,128)(2,1)}, u32[]{:S(2)}, u32[]{:S(2)}) %collective-permute-start) | collective-permute-done | bytes 1048608 | tf_op jit(solution)/shard_map/ppermute | solution.py:450
  39.4 2.2 collective-permute-start.2
  44.2 3.0 pad_maximum_fusion.1
  47.2 4.4 %collective-permute-done.5.refs_7_ = bf16[512,256]{1,0:T(8,128)(2,1)} collective-permute-done((bf16[512,256]{1,0:T(8,128)(2,1)S(1)}, bf16[512,256]{1,0:T(8,128)(2,1)}, u32[]{:S(2)}, u32[]{:S(2)}) %collective-permute-start.5) | collective-permute-done | bytes 262176 | tf_op jit(solution)/shard_map/ppermute | solution.py:450
  51.6 9.7 %collective-permute-done.2.refs_3_ = bf16[256,1024]{1,0:T(8,128)(2,1)S(1)} collective-permute-done((bf16[256,1024]{1,0:T(8,128)(2,1)S(1)}, bf16[256,1024]{1,0:T(8,128)(2,1)S(1)}, u32[]{:S(2)}, u32[]{:S(2)}) %collective-permute-start.2) | collective-permute-done | bytes 524320 | tf_op jit(solution)/shard_map/ppermute | solution.py:450
  65.1 2.6 collective-permute-start.10
  67.7 12.1 %project.1 = (bf16[2048,512]{1,0:T(8,128)(2,1)}, bf16[2048,512]{1,0:T(8,128)(2,1)}, bf16[2048,512]{1,0:T(8,128)(2,1)}, f32[8,256]{1,0:T(8,128)}, bf16[2048,1024]{1,0:T(8,128)(2,1)}) custom-call(s32[2]{0:T(128)} %pad_add_fusion.1.info_ref, bf16[512,1024]{1,0:T(8,128)(2,1)} %norm_rows.1.refs_0_, bf16[512,1024]{1,0:T(8,128)(2,1)} %collective-permute-done.refs_1_, ...), custom_call_target="tpu_custom_call" | custom-call | flops 3221225472 | bytes 17301504 | tf_op jit(solution)/shard_map/project/pallas_call | solution.py:132
  79.8 9.1 %collective-permute-done.9 = bf16[128,768]{1,0:T(8,128)(2,1)S(1)} collective-permute-done((bf16[128,768]{1,0:T(8,128)(2,1)S(1)}, bf16[128,768]{1,0:T(8,128)(2,1)S(1)}, u32[]{:S(2)}, u32[]{:S(2)}) %collective-permute-start.9) | collective-permute-done | bytes 196640 | tf_op jit(solution)/shard_map/ppermute | solution.py:450
  91.8 8.8 %attend.5 = (bf16[512,256]{1,0:T(8,128)(2,1)}, bf16[512,512]{1,0:T(8,128)(2,1)}) custom-call(s32[2]{0:T(128)} %pad_add_fusion.1.info_ref, s32[8]{0:T(128)} %and_select_fusion.begin_ref, bf16[2048,512]{1,0:T(8,128)(2,1)} %get-tuple-element.156.q_ref, bf16[2048,512]{1,0:T(8,128)(2,1)} %get-tuple-element.157.k_ref.refs_12_, ...), custom_call_target="tpu_custom_call" | custom-call | flops 1073741824 | bytes 4194304 | tf_op jit(solution)/shard_map/attend/pallas_call | solution.py:239
  100.6 8.8 %attend.6 = (bf16[512,256]{1,0:T(8,128)(2,1)}, bf16[512,512]{1,0:T(8,128)(2,1)}) custom-call(s32[2]{0:T(128)} %pad_add_fusion.1.info_ref, s32[8]{0:T(128)} %and_select_fusion.begin_ref, bf16[2048,512]{1,0:T(8,128)(2,1)} %get-tuple-element.156.q_ref, bf16[2048,512]{1,0:T(8,128)(2,1)} %get-tuple-element.157.k_ref.refs_12_, ...), custom_call_target="tpu_custom_call" | custom-call | flops 1073741824 | bytes 4194304 | tf_op jit(solution)/shard_map/attend/pallas_call | solution.py:239
  109.4 12.3 %attend.7 = (bf16[512,256]{1,0:T(8,128)(2,1)}, bf16[512,512]{1,0:T(8,128)(2,1)}) custom-call(s32[2]{0:T(128)} %pad_add_fusion.1.info_ref, s32[8]{0:T(128)} %and_select_fusion.begin_ref, bf16[2048,512]{1,0:T(8,128)(2,1)} %get-tuple-element.156.q_ref, bf16[2048,512]{1,0:T(8,128)(2,1)} %get-tuple-element.157.k_ref.refs_12_, ...), custom_call_target="tpu_custom_call" | custom-call | flops 1073741824 | bytes 4194304 | tf_op jit(solution)/shard_map/attend/pallas_call | solution.py:239
  121.7 3.5 collective-permute-start.14
  127.1 7.1 %attend.4 = (bf16[512,256]{1,0:T(8,128)(2,1)}, bf16[512,512]{1,0:T(8,128)(2,1)}) custom-call(s32[2]{0:T(128)} %pad_add_fusion.1.info_ref, s32[8]{0:T(128)} %and_select_fusion.begin_ref, bf16[2048,512]{1,0:T(8,128)(2,1)} %get-tuple-element.156.q_ref, bf16[2048,512]{1,0:T(8,128)(2,1)} %get-tuple-element.157.k_ref.refs_12_, ...), custom_call_target="tpu_custom_call" | custom-call | flops 1073741824 | bytes 4194304 | tf_op jit(solution)/shard_map/attend/pallas_call | solution.py:239
  134.3 2.3 collective-permute-done.14.refs_3_.refs_4_
  137.3 5.4 %branch.2 = (f32[256,1024]{1,0:T(8,128)}, bf16[256,1024]{1,0:T(8,128)(2,1)}) custom-call(s32[2]{0:T(128)} %pad_add_fusion.1.info_ref, bf16[512,256]{1,0:T(8,128)(2,1)} %get-tuple-element.171.refs_0_.refs_1_.refs_8_, bf16[512,256]{1,0:T(8,128)(2,1)} %copy-done.7, bf16[512,256]{1,0:T(8,128)(2,1)} %copy-done.8, bf16[512,256]{1,0:T(8,128)(2,1)} %copy-done.9, ...), custom_call_target="tpu_custom_call" | custom-call | flops 536870912 | bytes 4194304 | tf_op jit(solution)/shard_map/branch/pallas_call | solution.py:561
  143.4 5.5 %branch.3 = (f32[256,1024]{1,0:T(8,128)}, bf16[256,1024]{1,0:T(8,128)(2,1)}) custom-call(s32[2]{0:T(128)} %pad_add_fusion.1.info_ref, bf16[512,256]{1,0:T(8,128)(2,1)} %get-tuple-element.171.refs_0_.refs_1_.refs_8_, bf16[512,256]{1,0:T(8,128)(2,1)} %copy-done.7, bf16[512,256]{1,0:T(8,128)(2,1)} %copy-done.8, bf16[512,256]{1,0:T(8,128)(2,1)} %copy-done.9, ...), custom_call_target="tpu_custom_call" | custom-call | flops 536870912 | bytes 4194304 | tf_op jit(solution)/shard_map/branch/pallas_call | solution.py:561
  152.5 10.9 %feed.4 = (f32[512,1024]{1,0:T(8,128)}, f32[512,1024]{1,0:T(8,128)}, bf16[1,3,512,704]{3,2,1,0:T(8,128)(2,1)}) custom-call(s32[2]{0:T(128)} %pad_add_fusion.1.info_ref, bf16[512,1024]{1,0:T(8,128)(2,1)} %copy-done.22, bf16[512,1024]{1,0:T(8,128)(2,1)} %refs_7_.1, bf16[704,1024]{1,0:T(8,128)(2,1)} %bitcast.92, bf16[704,1024]{1,0:T(8,128)(2,1)} %bitcast.89, ...), custom_call_target="tpu_custom_call" | custom-call | flops 4429185024 | bytes 10616832 | tf_op jit(solution)/shard_map/feed/pallas_call | solution.py:674
  163.5 2.6 all-gather.8.cloned.1.call-done
  166.0 12.0 %feed.5 = (f32[512,1024]{1,0:T(8,128)}, f32[512,1024]{1,0:T(8,128)}, bf16[1,3,512,704]{3,2,1,0:T(8,128)(2,1)}) custom-call(s32[2]{0:T(128)} %pad_add_fusion.1.info_ref, bf16[512,1024]{1,0:T(8,128)(2,1)} %copy-done.22, bf16[512,1024]{1,0:T(8,128)(2,1)} %refs_7_.1, bf16[8,2112,128]{2,1,0:T(8,128)(2,1)} %bitcast.100, f32[512,1024]{1,0:T(8,128)} %get-tuple-element.179.refs_1_, ...), custom_call_target="tpu_custom_call" | custom-call | flops 4429185024 | bytes 10616832 | tf_op jit(solution)/shard_map/feed/pallas_call | solution.py:674
  178.8 11.5 %feed.6 = (bf16[256,1024]{1,0:T(8,128)(2,1)}, bf16[256,1024]{1,0:T(8,128)(2,1)}, bf16[2,3,256,704]{3,2,1,0:T(8,128)(2,1)}) custom-call(s32[2]{0:T(128)} %pad_add_fusion.1.info_ref, bf16[256,1024]{1,0:T(8,128)(2,1)} %copy-done.29, bf16[512,1024]{1,0:T(8,128)(2,1)} %collective-permute-done.11.g_ref.refs_4_.refs_5_, bf16[704,1024]{1,0:T(8,128)(2,1)} %bitcast.93, ...), custom_call_target="tpu_custom_call" | custom-call | flops 4429185024 | bytes 11796480 | tf_op jit(solution)/shard_map/feed/pallas_call | solution.py:674
  192.7 11.6 %feed.7 = (bf16[256,1024]{1,0:T(8,128)(2,1)}, bf16[256,1024]{1,0:T(8,128)(2,1)}, bf16[2,3,256,704]{3,2,1,0:T(8,128)(2,1)}) custom-call(s32[2]{0:T(128)} %pad_add_fusion.1.info_ref, bf16[256,1024]{1,0:T(8,128)(2,1)} %copy-done.30, bf16[512,1024]{1,0:T(8,128)(2,1)} %collective-permute-done.11.g_ref.refs_4_.refs_5_, bf16[704,1024]{1,0:T(8,128)(2,1)} %bitcast.94, ...), custom_call_target="tpu_custom_call" | custom-call | flops 4429185024 | bytes 11796480 | tf_op jit(solution)/shard_map/feed/pallas_call | solution.py:674
  204.9 10.9 %feed_grads.2 = (bf16[1,4,3,704,128]{4,3,2,1,0:T(8,128)(2,1)}, bf16[1,4,3,704,128]{4,3,2,1,0:T(8,128)(2,1)}) custom-call(s32[2]{0:T(128)} %pad_add_fusion.1.info_ref, bf16[512,1024]{1,0:T(8,128)(2,1)} %copy-done.22, bf16[256,1024]{1,0:T(8,128)(2,1)} %copy-done.29, bf16[256,1024]{1,0:T(8,128)(2,1)} %copy-done.30, bf16[512,1024]{1,0:T(8,128)(2,1)} %refs_7_.1, ...), custom_call_target="tpu_custom_call" | custom-call | flops 4429185024 | bytes 8650752 | tf_op jit(solution)/shard_map/feed_grads/pallas_call | solution.py:738
  215.7 10.7 %feed_grads.3 = (bf16[1,4,3,704,128]{4,3,2,1,0:T(8,128)(2,1)}, bf16[1,4,3,704,128]{4,3,2,1,0:T(8,128)(2,1)}) custom-call(s32[2]{0:T(128)} %pad_add_fusion.1.info_ref, bf16[512,1024]{1,0:T(8,128)(2,1)} %copy-done.22, bf16[256,1024]{1,0:T(8,128)(2,1)} %copy-done.29, bf16[256,1024]{1,0:T(8,128)(2,1)} %copy-done.30, bf16[512,1024]{1,0:T(8,128)(2,1)} %refs_7_.1, ...), custom_call_target="tpu_custom_call" | custom-call | flops 4429185024 | bytes 8650752 | tf_op jit(solution)/shard_map/feed_grads/pallas_call | solution.py:738
  227.1 2.1 pad_maximum_fusion.3
  229.7 7.6 %branch_back.1 = (f32[512,1024]{1,0:T(8,128)}, bf16[512,1024]{1,0:T(8,128)(2,1)}, f32[1,1024]{1,0:T(1,128)}, bf16[512,256]{1,0:T(8,128)(2,1)}, bf16[512,256]{1,0...) custom-call(s32[2]{0:T(128)} %pad_add_fusion.1.info_ref, ...), custom_call_target="tpu_custom_call" | custom-call | flops 1073741824 | bytes 12582912 | tf_op jit(solution)/shard_map/branch_back/pallas_call | solution.py:802
  240.7 4.8 %out_grads.1 = bf16[1024,1024]{1,0:T(8,128)(2,1)} custom-call(s32[2]{0:T(128)} %pad_add_fusion.1.info_ref, bf16[512,1024]{1,0:T(8,128)(2,1)} %get-tuple-element.211.refs_0_, bf16[512,256]{1,0:T(8,128)(2,1)} %get-tuple-element.171.refs_0_.refs_1_.refs_8_, bf16[512,256]{1,0:T(8,128)(2,1)} %copy-done.7, bf16[512,256]{1,0:T(8,128)(2,1)} %copy-done.8, ...), custom_call_target="tpu_custom_call" | custom-call | flops 1073741824 | bytes 5242880 | tf_op jit(solution)/shard_map/out_grads/pallas_call | solution.py:843
  245.5 2.0 fusion.12
  249.6 3.1 fusion.5
  254.8 2.5 copy.41
  263.5 2.5 collective-permute-start.25
  267.3 45.8 %attend_back.1 = (bf16[2048,768]{1,0:T(8,128)(2,1)}, bf16[512,768]{1,0:T(8,128)(2,1)}, bf16[512,768]{1,0:T(8,128)(2,1)}, bf16[512,768]{1,0:T(8,128)(2,1)}, bf16[512,768]{1,0:T(8,128)(2,1)}) custom-call(s32[2]{0:T(128)} %pad_add_fusion.1.info_ref, s32[8]{0:T(128)} %and_select_fusion.begin_ref, bf16[512,512]{1,0:T(8,128)(2,1)} %get-tuple-element.159.refs_0_, ...), custom_call_target="tpu_custom_call" | custom-call | flops 10737418240 | bytes 16777216 | tf_op jit(solution)/shard_map/attend_back/pallas_call | solution.py:407
  314.6 1.8 copy.42
  316.5 2.8 add_convert_fusion
  319.4 10.7 %qkv_grads.1 = (bf16[1024,768]{1,0:T(8,128)(2,1)}, f32[1024,1]{1,0:T(8,128)}) custom-call(bf16[2048,1024]{1,0:T(8,128)(2,1)} %get-tuple-element.237.x_ref, bf16[2048,768]{1,0:T(8,128)(2,1)} %get-tuple-element.238.d_ref, bf16[1024,768]{1,0:T(8,128)(2,1)} %bitcast.88, bf16[768,768]{1,0:T(8,128)(2,1)} %fusion.sel_ref), custom_call_target="tpu_custom_call" | custom-call | flops 3221225472 | bytes 10485760 | tf_op jit(solution)/shard_map/qkv_grads/pallas_call | solution.py:874
  335.6 3.5 collective-permute-start.32
  341.6 3.4 fusion.3
  345.2 27.7 %collective-permute-done.33 = bf16[704,128]{1,0:T(8,128)(2,1)S(1)} collective-permute-done((bf16[704,128]{1,0:T(8,128)(2,1)S(1)}, bf16[704,128]{1,0:T(8,128)(2,1)S(1)}, u32[]{:S(2)}, u32[]{:S(2)}) %collective-permute-start.33) | collective-permute-done | bytes 180256 | tf_op jit(solution)/shard_map/ppermute | solution.py:450
  376.3 2.6 collective-permute-done.34
  378.9 2.3 collective-permute-start.35
  381.2 1.7 collective-permute-done.35
  384.2 4.0 collective-permute-start.37
  389.9 2.1 collective-permute-start.38
  392.0 10.5 %finish.1 = (f32[512,1024]{1,0:T(8,128)}, f32[512,1024]{1,0:T(8,128)}) custom-call(s32[2]{0:T(128)} %pad_add_fusion.1.info_ref, bf16[512,768]{1,0:T(8,128)(2,1)} %get-tuple-element.249.refs_0_, bf16[512,768]{1,0:T(8,128)(2,1)} %collective-permute-done.29.refs_1_, bf16[512,768]{1,0:T(8,128)(2,1)} %collective-permute-done.30.refs_2_, ...), custom_call_target="tpu_custom_call" | custom-call | flops 3221225472 | bytes 14680064 | tf_op jit(solution)/shard_map/finish/pallas_call | solution.py:949
  402.6 5.0 %collective-permute-done.38 = f32[3,1024]{1,0:T(4,128)S(1)} collective-permute-done((f32[3,1024]{1,0:T(4,128)S(1)}, f32[3,1024]{1,0:T(4,128)S(1)}, u32[]{:S(2)}, u32[]{:S(2)}) %collective-permute-start.38) | collective-permute-done | bytes 12320 | tf_op jit(solution)/shard_map/ppermute | solution.py:450
  (193 shorter events, 66.1 us)
Async XLA Ops:
  7.2 119.9 %all-gather.6.cloned.1.call-start = ((), (), s32[]{:S(2)}) async-start(), calls=%async_computation.3 | async-start | bytes 2621440 | tf_op jit(solution)/shard_map/all_gather | solution.py:1051
  11.1 27.2 %collective-permute-start = (bf16[512,1024]{1,0:T(8,128)(2,1)}, bf16[512,1024]{1,0:T(8,128)(2,1)}, u32[]{:S(2)}, u32[]{:S(2)}) collective-permute-start(bf16[512,1024]{1,0:T(8,128)(2,1)} %norm_rows.1.refs_0_), channel_id=1, source_target_pairs={{0,1},{1,0},{2,3},{3,2},{4,5},{5,4},{6,7},{7,6},{8,9},{9,8},{10,11... | collective-permute-start | bytes 3145736 | tf_op jit(solution)/shard_map/ppermute | solution.py:450
  14.0 27.5 %collective-permute-start.1 = (bf16[512,1024]{1,0:T(8,128)(2,1)}, bf16[512,1024]{1,0:T(8,128)(2,1)}, u32[]{:S(2)}, u32[]{:S(2)}) collective-permute-start(bf16[512,1024]{1,0:T(8,128)(2,1)} %norm_rows.1.refs_0_), channel_id=1, source_target_pairs={{0,2},{1,3},{2,0},{3,1},{4,6},{5,7},{6,4},{7,5},{8,10},{9,11},{10,... | collective-permute-start | bytes 3145736 | tf_op jit(solution)/shard_map/ppermute | solution.py:450
  16.4 30.9 %collective-permute-start.4 = (bf16[512,256]{1,0:T(8,128)(2,1)S(1)}, bf16[512,256]{1,0:T(8,128)(2,1)S(1)}, u32[]{:S(2)}, u32[]{:S(2)}) collective-permute-start(bf16[512,256]{1,0:T(8,128)(2,1)S(1)} %get-tuple-element.266), channel_id=1, source_target_pairs={{0,1},{1,0},{2,3},{3,2},{4,5},{5,4},{6,7},{7,6},{8,9},{9,8},{10,11... | collective-permute-start | bytes 786440 | tf_op jit(solution)/shard_map/ppermute | solution.py:450
  16.9 34.7 %collective-permute-start.5 = (bf16[512,256]{1,0:T(8,128)(2,1)S(1)}, bf16[512,256]{1,0:T(8,128)(2,1)}, u32[]{:S(2)}, u32[]{:S(2)}) collective-permute-start(bf16[512,256]{1,0:T(8,128)(2,1)S(1)} %get-tuple-element.268), channel_id=1, source_target_pairs={{0,2},{1,3},{2,0},{3,1},{4,6},{5,7},{6,4},{7,5},{8,10},{9,11},{10,... | collective-permute-start | bytes 786440 | tf_op jit(solution)/shard_map/ppermute | solution.py:450
  16.9 34.7 %collective-permute-start.6 = (bf16[512,256]{1,0:T(8,128)(2,1)S(1)}, bf16[512,256]{1,0:T(8,128)(2,1)}, u32[]{:S(2)}, u32[]{:S(2)}) collective-permute-start(bf16[512,256]{1,0:T(8,128)(2,1)S(1)} %get-tuple-element.265), channel_id=1, source_target_pairs={{0,3},{1,2},{2,1},{3,0},{4,7},{5,6},{6,5},{7,4},{8,11},{9,10},{10,... | collective-permute-start | bytes 786440 | tf_op jit(solution)/shard_map/ppermute | solution.py:450
  39.4 21.9 %collective-permute-start.2 = (bf16[256,1024]{1,0:T(8,128)(2,1)S(1)}, bf16[256,1024]{1,0:T(8,128)(2,1)S(1)}, u32[]{:S(2)}, u32[]{:S(2)}) collective-permute-start(bf16[256,1024]{1,0:T(8,128)(2,1)S(1)} %slice.76), channel_id=1, source_target_pairs={{0,2},{1,3},{2,0},{3,1},{4,6},{5,7},{6,4},{7,5},{8,10},{9,11},{10,... | collective-permute-start | bytes 1572872 | tf_op jit(solution)/shard_map/ppermute | solution.py:450
  42.6 18.7 %collective-permute-start.3 = (bf16[256,1024]{1,0:T(8,128)(2,1)S(1)}, bf16[256,1024]{1,0:T(8,128)(2,1)S(1)}, u32[]{:S(2)}, u32[]{:S(2)}) collective-permute-start(bf16[256,1024]{1,0:T(8,128)(2,1)S(1)} %slice.77), channel_id=1, source_target_pairs={{0,1},{1,0},{2,3},{3,2},{4,5},{5,4},{6,7},{7,6},{8,9},{9,8},{10,11... | collective-permute-start | bytes 1572872 | tf_op jit(solution)/shard_map/ppermute | solution.py:450
  62.1 103.9 %all-gather.8.cloned.1.call-start = ((), (), s32[]{:S(2)}) async-start(), calls=%async_computation.6 | async-start | bytes 4866048 | tf_op jit(solution)/shard_map/all_gather | solution.py:1061
  62.1 26.9 %collective-permute-start.7 = (bf16[2112,128]{1,0:T(8,128)(2,1)S(1)}, bf16[2112,128]{1,0:T(8,128)(2,1)S(1)}, u32[]{:S(2)}, u32[]{:S(2)}) collective-permute-start(bf16[2112,128]{1,0:T(8,128)(2,1)S(1)} %pad_maximum_fusion.5), channel_id=1, source_target_pairs={{0,2},{1,3},{2,0},{3,1},{4,6},{5,7},{6,4},{7,5},{8,10},{9,11},{10,... | collective-permute-start | bytes 1622024 | tf_op jit(solution)/shard_map/ppermute | solution.py:450
  64.2 26.1 %copy-start.14 = (bf16[512,1024]{1,0:T(8,128)(2,1)S(1)}, bf16[512,1024]{1,0:T(8,128)(2,1)}, u32[]{:S(2)}) copy-start(bf16[512,1024]{1,0:T(8,128)(2,1)} %refs_7_.1) | copy-start | bytes 3145732
  64.2 15.6 %collective-permute-start.8 = (bf16[128,768]{1,0:T(8,128)(2,1)S(1)}, bf16[128,768]{1,0:T(8,128)(2,1)S(1)}, u32[]{:S(2)}, u32[]{:S(2)}) collective-permute-start(bf16[128,768]{1,0:T(8,128)(2,1)S(1)} %dynamic-slice_bitcast_fusion.4), channel_id=1, source_target_pairs={{0,1},{1,0},{2,3},{3,2},{4,5},{5,4},{6,7},{7,6},{8,9},{9,8},{10,11... | collective-permute-start | bytes 589832 | tf_op jit(solution)/shard_map/ppermute | solution.py:450
  64.7 24.2 %collective-permute-start.9 = (bf16[128,768]{1,0:T(8,128)(2,1)S(1)}, bf16[128,768]{1,0:T(8,128)(2,1)S(1)}, u32[]{:S(2)}, u32[]{:S(2)}) collective-permute-start(bf16[128,768]{1,0:T(8,128)(2,1)S(1)} %dynamic-slice_bitcast_fusion.4), channel_id=1, source_target_pairs={{0,2},{1,3},{2,0},{3,1},{4,6},{5,7},{6,4},{7,5},{8,10},{9,11},{10,... | collective-permute-start | bytes 589832 | tf_op jit(solution)/shard_map/ppermute | solution.py:450
  65.1 23.9 %collective-permute-start.10 = (bf16[128,768]{1,0:T(8,128)(2,1)S(1)}, bf16[128,768]{1,0:T(8,128)(2,1)S(1)}, u32[]{:S(2)}, u32[]{:S(2)}) collective-permute-start(bf16[128,768]{1,0:T(8,128)(2,1)S(1)} %dynamic-slice_bitcast_fusion.4), channel_id=1, source_target_pairs={{0,3},{1,2},{2,1},{3,0},{4,7},{5,6},{6,5},{7,4},{8,11},{9,10},{10,... | collective-permute-start | bytes 589832 | tf_op jit(solution)/shard_map/ppermute | solution.py:450
  89.8 223.4 %all-gather.10.cloned.1.call-start = ((), (), s32[]{:S(2)}) async-start(), calls=%async_computation.7 | async-start | bytes 7077888 | tf_op jit(solution)/shard_map/all_gather | solution.py:1072
  90.4 36.8 %collective-permute-start.11 = (bf16[512,1024]{1,0:T(8,128)(2,1)S(1)}, bf16[512,1024]{1,0:T(8,128)(2,1)}, u32[]{:S(2)}, u32[]{:S(2)}) collective-permute-start(bf16[512,1024]{1,0:T(8,128)(2,1)S(1)} %copy-done.14), channel_id=1, source_target_pairs={{0,1},{1,0},{2,3},{3,2},{4,5},{5,4},{6,7},{7,6},{8,9},{9,8},{10,11... | collective-permute-start | bytes 3145736 | tf_op jit(solution)/shard_map/ppermute | solution.py:450
  100.6 33.7 %collective-permute-start.12 = (bf16[512,256]{1,0:T(8,128)(2,1)}, bf16[512,256]{1,0:T(8,128)(2,1)S(1)}, u32[]{:S(2)}, u32[]{:S(2)}) collective-permute-start(bf16[512,256]{1,0:T(8,128)(2,1)} %get-tuple-element.164.refs_9_), channel_id=1, source_target_pairs={{0,1},{1,0},{2,3},{3,2},{4,5},{5,4},{6,7},{7,6},{8,9},{9,8},{10,11... | collective-permute-start | bytes 786440 | tf_op jit(solution)/shard_map/ppermute | solution.py:450
  121.7 12.6 %collective-permute-start.13 = (bf16[512,256]{1,0:T(8,128)(2,1)S(1)}, bf16[512,256]{1,0:T(8,128)(2,1)S(1)}, u32[]{:S(2)}, u32[]{:S(2)}) collective-permute-start(bf16[512,256]{1,0:T(8,128)(2,1)S(1)} %copy-done.31), channel_id=1, source_target_pairs={{0,2},{1,3},{2,0},{3,1},{4,6},{5,7},{6,4},{7,5},{8,10},{9,11},{10,... | collective-permute-start | bytes 786440 | tf_op jit(solution)/shard_map/ppermute | solution.py:450
  121.7 14.9 %collective-permute-start.14 = (bf16[512,256]{1,0:T(8,128)(2,1)}, bf16[512,256]{1,0:T(8,128)(2,1)S(1)}, u32[]{:S(2)}, u32[]{:S(2)}) collective-permute-start(bf16[512,256]{1,0:T(8,128)(2,1)} %get-tuple-element.166.refs_11_), channel_id=1, source_target_pairs={{0,3},{1,2},{2,1},{3,0},{4,7},{5,6},{6,5},{7,4},{8,11},{9,10},{10,... | collective-permute-start | bytes 786440 | tf_op jit(solution)/shard_map/ppermute | solution.py:450
  136.7 178.0 %reduce-scatter.10.cloned.1.call-start = ((), (), s32[]{:S(2)}) async-start(), calls=%async_computation.8 | async-start | bytes 2359296
  142.8 35.2 %collective-permute-start.15 = (bf16[256,1024]{1,0:T(8,128)(2,1)}, bf16[256,1024]{1,0:T(8,128)(2,1)S(1)}, u32[]{:S(2)}, u32[]{:S(2)}) collective-permute-start(bf16[256,1024]{1,0:T(8,128)(2,1)} %get-tuple-element.176), channel_id=1, source_target_pairs={{0,1},{1,0},{2,3},{3,2},{4,5},{5,4},{6,7},{7,6},{8,9},{9,8},{10,11... | collective-permute-start | bytes 1572872 | tf_op jit(solution)/shard_map/ppermute | solution.py:450
  148.8 43.0 %collective-permute-start.17 = (bf16[256,1024]{1,0:T(8,128)(2,1)}, bf16[256,1024]{1,0:T(8,128)(2,1)S(1)}, u32[]{:S(2)}, u32[]{:S(2)}) collective-permute-start(bf16[256,1024]{1,0:T(8,128)(2,1)} %get-tuple-element.177), channel_id=1, source_target_pairs={{0,1},{1,0},{2,3},{3,2},{4,5},{5,4},{6,7},{7,6},{8,9},{9,8},{10,11... | collective-permute-start | bytes 1572872 | tf_op jit(solution)/shard_map/ppermute | solution.py:450
  190.3 36.2 %collective-permute-start.16 = (bf16[256,1024]{1,0:T(8,128)(2,1)}, bf16[256,1024]{1,0:T(8,128)(2,1)S(1)}, u32[]{:S(2)}, u32[]{:S(2)}) collective-permute-start(bf16[256,1024]{1,0:T(8,128)(2,1)} %get-tuple-element.185), channel_id=1, source_target_pairs={{0,1},{1,0},{2,3},{3,2},{4,5},{5,4},{6,7},{7,6},{8,9},{9,8},{10,11... | collective-permute-start | bytes 1572872 | tf_op jit(solution)/shard_map/ppermute | solution.py:450
  204.2 22.3 %collective-permute-start.18 = (bf16[256,1024]{1,0:T(8,128)(2,1)}, bf16[256,1024]{1,0:T(8,128)(2,1)S(1)}, u32[]{:S(2)}, u32[]{:S(2)}) collective-permute-start(bf16[256,1024]{1,0:T(8,128)(2,1)} %get-tuple-element.188), channel_id=1, source_target_pairs={{0,1},{1,0},{2,3},{3,2},{4,5},{5,4},{6,7},{7,6},{8,9},{9,8},{10,11... | collective-permute-start | bytes 1572872 | tf_op jit(solution)/shard_map/ppermute | solution.py:450
  226.5 19.0 %collective-permute-start.23 = (bf16[1,4,3,704,128]{4,3,2,1,0:T(8,128)(2,1)}, bf16[1,4,3,704,128]{4,3,2,1,0:T(8,128)(2,1)S(1)}, u32[]{:S(2)}, u32[]{:S(2)}) collective-permute-start(bf16[1,4,3,704,128]{4,3,2,1,0:T(8,128)(2,1)} %get-tuple-element.208), channel_id=1, source_target_pairs={{0,4},{4,0},{8,12},{12,8},{16,20},{20,16},{24,28},{28,24},{1,5},{5... | collective-permute-start | bytes 6488072 | tf_op jit(solution)/shard_map/ppermute | solution.py:450
  226.6 20.9 %collective-permute-start.22 = (bf16[1,4,3,704,128]{4,3,2,1,0:T(8,128)(2,1)}, bf16[1,4,3,704,128]{4,3,2,1,0:T(8,128)(2,1)}, u32[]{:S(2)}, u32[]{:S(2)}) collective-permute-start(bf16[1,4,3,704,128]{4,3,2,1,0:T(8,128)(2,1)} %get-tuple-element.206), channel_id=1, source_target_pairs={{0,4},{4,0},{8,12},{12,8},{16,20},{20,16},{24,28},{28,24},{1,5},{5... | collective-permute-start | bytes 6488072 | tf_op jit(solution)/shard_map/ppermute | solution.py:450
  237.3 16.9 %collective-permute-start.19 = (bf16[512,256]{1,0:T(8,128)(2,1)}, bf16[512,256]{1,0:T(8,128)(2,1)}, u32[]{:S(2)}, u32[]{:S(2)}) collective-permute-start(bf16[512,256]{1,0:T(8,128)(2,1)} %get-tuple-element.202), channel_id=1, source_target_pairs={{0,1},{1,0},{2,3},{3,2},{4,5},{5,4},{6,7},{7,6},{8,9},{9,8},{10,11... | collective-permute-start | bytes 786440 | tf_op jit(solution)/shard_map/ppermute | solution.py:450
  238.7 15.4 %collective-permute-start.20 = (bf16[512,256]{1,0:T(8,128)(2,1)}, bf16[512,256]{1,0:T(8,128)(2,1)}, u32[]{:S(2)}, u32[]{:S(2)}) collective-permute-start(bf16[512,256]{1,0:T(8,128)(2,1)} %get-tuple-element.203), channel_id=1, source_target_pairs={{0,2},{1,3},{2,0},{3,1},{4,6},{5,7},{6,4},{7,5},{8,10},{9,11},{10,... | collective-permute-start | bytes 786440 | tf_op jit(solution)/shard_map/ppermute | solution.py:450
  240.2 14.0 %collective-permute-start.21 = (bf16[512,256]{1,0:T(8,128)(2,1)}, bf16[512,256]{1,0:T(8,128)(2,1)}, u32[]{:S(2)}, u32[]{:S(2)}) collective-permute-start(bf16[512,256]{1,0:T(8,128)(2,1)} %get-tuple-element.204), channel_id=1, source_target_pairs={{0,3},{1,2},{2,1},{3,0},{4,7},{5,6},{6,5},{7,4},{8,11},{9,10},{10,... | collective-permute-start | bytes 786440 | tf_op jit(solution)/shard_map/ppermute | solution.py:450
  257.3 153.8 %reduce-scatter.8.cloned.1.call-start = ((), (), s32[]{:S(2)}) async-start(), calls=%async_computation.5 | async-start | bytes 327680 | tf_op jit(solution)/shard_map/reduce_scatter | solution.py:1176
  257.6 55.5 %collective-permute-start.27 = (bf16[4,2,704,128]{3,2,1,0:T(8,128)(2,1)}, bf16[4,2,704,128]{3,2,1,0:T(8,128)(2,1)}, u32[]{:S(2)}, u32[]{:S(2)}) collective-permute-start(bf16[4,2,704,128]{3,2,1,0:T(8,128)(2,1)} %fusion.6), channel_id=1, source_target_pairs={{0,2},{1,3},{2,0},{3,1},{4,6},{5,7},{6,4},{7,5},{8,10},{9,11},{10,... | collective-permute-start | bytes 4325384 | tf_op jit(solution)/shard_map/ppermute | solution.py:450
  260.6 52.5 %collective-permute-start.28 = (bf16[512,1024]{1,0:T(8,128)(2,1)}, bf16[512,1024]{1,0:T(8,128)(2,1)}, u32[]{:S(2)}, u32[]{:S(2)}) collective-permute-start(bf16[512,1024]{1,0:T(8,128)(2,1)} %pad_maximum_fusion.3), channel_id=1, source_target_pairs={{0,1},{1,0},{2,3},{3,2},{4,5},{5,4},{6,7},{7,6},{8,9},{9,8},{10,11... | collective-permute-start | bytes 3145736 | tf_op jit(solution)/shard_map/ppermute | solution.py:450
  262.9 50.2 %collective-permute-start.24 = (bf16[2,704,128]{2,1,0:T(8,128)(2,1)}, bf16[2,704,128]{2,1,0:T(8,128)(2,1)}, u32[]{:S(2)}, u32[]{:S(2)}) collective-permute-start(bf16[2,704,128]{2,1,0:T(8,128)(2,1)} %get-tuple-element.264), channel_id=1, source_target_pairs={{0,8},{4,12},{8,0},{12,4},{16,24},{20,28},{24,16},{28,20},{1,9},{5... | collective-permute-start | bytes 1081352 | tf_op jit(solution)/shard_map/ppermute | solution.py:450
  263.5 49.6 %collective-permute-start.25 = (bf16[2,704,128]{2,1,0:T(8,128)(2,1)S(1)}, bf16[2,704,128]{2,1,0:T(8,128)(2,1)}, u32[]{:S(2)}, u32[]{:S(2)}) collective-permute-start(bf16[2,704,128]{2,1,0:T(8,128)(2,1)S(1)} %get-tuple-element.263), channel_id=1, source_target_pairs={{0,16},{4,20},{8,24},{12,28},{16,0},{20,4},{24,8},{28,12},{1,17},{... | collective-permute-start | bytes 1081352 | tf_op jit(solution)/shard_map/ppermute | solution.py:450
  266.0 47.1 %collective-permute-start.26 = (bf16[2,704,128]{2,1,0:T(8,128)(2,1)S(1)}, bf16[2,704,128]{2,1,0:T(8,128)(2,1)}, u32[]{:S(2)}, u32[]{:S(2)}) collective-permute-start(bf16[2,704,128]{2,1,0:T(8,128)(2,1)S(1)} %get-tuple-element.262), channel_id=1, source_target_pairs={{0,24},{4,28},{8,16},{12,20},{16,8},{20,12},{24,0},{28,4},{1,25},{... | collective-permute-start | bytes 1081352 | tf_op jit(solution)/shard_map/ppermute | solution.py:450
  267.3 49.2 %copy-start.3 = (bf16[4,2,704,128]{3,2,1,0:T(8,128)(2,1)S(1)}, bf16[4,2,704,128]{3,2,1,0:T(8,128)(2,1)}, u32[]{:S(2)}) copy-start(bf16[4,2,704,128]{3,2,1,0:T(8,128)(2,1)} %fusion.5) | copy-start | bytes 4325380
  316.5 96.2 %reduce-scatter.6.cloned.1.call-start = ((), (), s32[]{:S(2)}) async-start(), calls=%async_computation.4 | async-start | bytes 1769472 | tf_op jit(solution)/shard_map/reduce_scatter | solution.py:1159
  331.1 44.0 %collective-permute-start.29 = (bf16[512,768]{1,0:T(8,128)(2,1)}, bf16[512,768]{1,0:T(8,128)(2,1)}, u32[]{:S(2)}, u32[]{:S(2)}) collective-permute-start(bf16[512,768]{1,0:T(8,128)(2,1)} %get-tuple-element.234), channel_id=1, source_target_pairs={{0,1},{1,0},{2,3},{3,2},{4,5},{5,4},{6,7},{7,6},{8,9},{9,8},{10,11... | collective-permute-start | bytes 2359304 | tf_op jit(solution)/shard_map/ppermute | solution.py:450
  332.3 42.8 %collective-permute-start.30 = (bf16[512,768]{1,0:T(8,128)(2,1)}, bf16[512,768]{1,0:T(8,128)(2,1)}, u32[]{:S(2)}, u32[]{:S(2)}) collective-permute-start(bf16[512,768]{1,0:T(8,128)(2,1)} %get-tuple-element.235), channel_id=1, source_target_pairs={{0,2},{1,3},{2,0},{3,1},{4,6},{5,7},{6,4},{7,5},{8,10},{9,11},{10,... | collective-permute-start | bytes 2359304 | tf_op jit(solution)/shard_map/ppermute | solution.py:450
  333.8 41.2 %collective-permute-start.31 = (bf16[512,768]{1,0:T(8,128)(2,1)}, bf16[512,768]{1,0:T(8,128)(2,1)}, u32[]{:S(2)}, u32[]{:S(2)}) collective-permute-start(bf16[512,768]{1,0:T(8,128)(2,1)} %get-tuple-element.236), channel_id=1, source_target_pairs={{0,3},{1,2},{2,1},{3,0},{4,7},{5,6},{6,5},{7,4},{8,11},{9,10},{10,... | collective-permute-start | bytes 2359304 | tf_op jit(solution)/shard_map/ppermute | solution.py:450
  335.6 38.2 %collective-permute-start.32 = (bf16[2,2,704,128]{3,2,1,0:T(8,128)(2,1)}, bf16[2,2,704,128]{3,2,1,0:T(8,128)(2,1)}, u32[]{:S(2)}, u32[]{:S(2)}) collective-permute-start(bf16[2,2,704,128]{3,2,1,0:T(8,128)(2,1)} %dynamic-slice_bitcast_fusion), channel_id=1, source_target_pairs={{0,8},{4,12},{8,0},{12,4},{16,24},{20,28},{24,16},{28,20},{1,9},{5... | collective-permute-start | bytes 2162696 | tf_op jit(solution)/shard_map/ppermute | solution.py:450
  340.5 32.5 %collective-permute-start.33 = (bf16[704,128]{1,0:T(8,128)(2,1)S(1)}, bf16[704,128]{1,0:T(8,128)(2,1)S(1)}, u32[]{:S(2)}, u32[]{:S(2)}) collective-permute-start(bf16[704,128]{1,0:T(8,128)(2,1)S(1)} %slice_bitcast_fusion.3), channel_id=1, source_target_pairs={{0,2},{1,3},{2,0},{3,1},{4,6},{5,7},{6,4},{7,5},{8,10},{9,11},{10,... | collective-permute-start | bytes 540680 | tf_op jit(solution)/shard_map/ppermute | solution.py:450
  375.1 3.8 collective-permute-start.34
  378.9 4.0 collective-permute-start.35
  383.0 1.2 collective-permute-start.36
  384.2 5.7 %collective-permute-start.37 = (f32[3,1024]{1,0:T(4,128)S(1)}, f32[3,1024]{1,0:T(4,128)S(1)}, u32[]{:S(2)}, u32[]{:S(2)}) collective-permute-start(f32[3,1024]{1,0:T(4,128)S(1)} %add.172), channel_id=1, source_target_pairs={{0,8},{4,12},{8,0},{12,4},{16,24},{20,28},{24,16},{28,20},{1,9},{5... | collective-permute-start | bytes 36872 | tf_op jit(solution)/shard_map/ppermute | solution.py:450
  388.2 22.0 %collective-permute-start.39 = (bf16[1,2,704,128]{3,2,1,0:T(8,128)(2,1)S(1)}, bf16[1,2,704,128]{3,2,1,0:T(8,128)(2,1)S(1)}, u32[]{:S(2)}, u32[]{:S(2)}) collective-permute-start(bf16[1,2,704,128]{3,2,1,0:T(8,128)(2,1)S(1)} %constant_dynamic-slice_fusion), channel_id=1, source_target_pairs={{0,16},{4,20},{8,24},{12,28},{16,0},{20,4},{24,8},{28,12},{1,17},{... | collective-permute-start | bytes 1081352 | tf_op jit(solution)/shard_map/ppermute | solution.py:450
  389.9 17.7 %collective-permute-start.38 = (f32[3,1024]{1,0:T(4,128)S(1)}, f32[3,1024]{1,0:T(4,128)S(1)}, u32[]{:S(2)}, u32[]{:S(2)}) collective-permute-start(f32[3,1024]{1,0:T(4,128)S(1)} %add.173), channel_id=1, source_target_pairs={{0,16},{4,20},{8,24},{12,28},{16,0},{20,4},{24,8},{28,12},{1,17},{... | collective-permute-start | bytes 36872 | tf_op jit(solution)/shard_map/ppermute | solution.py:450
  (32 other events, 210.6 us)
Sparse Core Ops, SparseCore 0:
  61.5 54.5 all-gather.5
  117.7 48.3 all-gather.7
  167.7 65.9 all-gather.9
  257.4 57.1 reduce-scatter.9
  317.8 26.9 reduce-scatter.7
  347.1 34.1 reduce-scatter.5
